TPU v7x, 32 devices: a whole 2x2x4 slice. The times are simulated.
32 devices in a mesh: rows: 8 (over z, y), cols: 4 (over x, core).
Axes of the slice: x: 2, y: 2, z: 4, core: 2. Of those that a mesh axis runs over, the one named last changes fastest.
Arguments:
- sketch: float32 [32768, 256], P(('rows', 'cols'))
- tiles: bfloat16 [1280, 512, 512], P(('rows', 'cols')), may hold values from -48 to 48
- tile_user: int32 [1280], P(('rows', 'cols')), may hold values from 0 to 7
- tile_item: int32 [1280], P(('rows', 'cols')), may hold values from 0 to 7
- tile_count: int32 [32], P(('rows', 'cols')), may hold values from 5 to 40, as said below
- item_owner: int32 [4, 8], P('cols'), may hold values from 0 to 7, each once within a row
Outputs:
- projected: float32 [8, 4, 256, 512], P('rows', 'cols')
Inputs may be any that keep to these rules, and one draw needn't show every extreme that they name: `tile_count`: live slots of a device are its first slots; some device has all 40 live in every draw.
All inputs are finite; a program needn't handle non-finite values.
Results may differ from a plain program's by a relative error of at most 0.0029.
Values may be sent and summed in bfloat16 or wider, within the bound.
No kernel may reach another device: no remote copies, remote signals or barrier semaphores. Data moves between devices by JAX's collectives and lax.ppermute only.
A program may use at most 192 MiB of HBM per device.

v0:
```python
import functools

import jax
import jax.numpy as jnp
from jax import lax
from jax.experimental import pallas as pl
from jax.experimental.pallas import tpu as pltpu
from jax.sharding import PartitionSpec as P

F32 = jnp.float32
BF16 = jnp.bfloat16
HIGH = lax.Precision.HIGHEST
SLOTS = 12
GROUP = 4
NEAR_COST = 200 * 2**20
EARLY_COST = 1024
LATE_COST = 1024
FACTOR_COST = 200 * 2**20
CHUNKS = 2
NEWTON = 2


def bits_of(count):
    return [1 << b for b in reversed(range(count.bit_length() - 1))]


def swap(x, axis, count, bit):
    return lax.ppermute(x, axis, [(i, i ^ bit) for i in range(count)])


def places(order, parity):
    found = [parity << order[0]]
    for bit in reversed(order[1:]):
        found = found + [p | (1 << bit) for p in found]
    return found


def run_tiles(base, span, per_piece, users, items, owner, meta, tiles, slab, add, buf, sems, order):
    count, row, col = meta[0], meta[1], meta[2]

    def relative(t):
        user = users[t]
        return lax.bitwise_xor(user // per_piece, col) - base, lax.rem(user, per_piece)

    def choose(t, n):
        piece, _ = relative(t)
        order[n] = t
        return n + jnp.where((piece >= 0) & (piece < span), 1, 0)

    live = lax.fori_loop(0, count, choose, 0)

    def fetch(i):
        slot = lax.rem(i, SLOTS)
        return pltpu.make_async_copy(tiles.at[order[i]], buf.at[slot], sems.at[slot])

    for i in range(SLOTS):
        @pl.when(i < live)
        def _():
            fetch(i).start()

    def group(first, size):
        for q in range(size):
            fetch(first + q).wait()
        found = []
        for q in range(size):
            piece, part = relative(order[first + q])
            both = jnp.dot(
                slab[piece * per_piece + part],
                buf[lax.rem(first + q, SLOTS)],
                preferred_element_type=F32,
            )
            half = both.shape[0] // 2
            found.append(both[:half] + both[half:])
        for q in range(size):
            add(lax.bitwise_xor(owner[items[order[first + q]]], row), found[q])
        for q in range(size):
            @pl.when(first + q + SLOTS < live)
            def _():
                fetch(first + q + SLOTS).start()

    def finish():
        groups = live // GROUP

        def many(g, _):
            group(g * GROUP, GROUP)
            return 0

        def one(i, _):
            group(i, 1)
            return 0

        lax.fori_loop(0, groups, many, 0)
        lax.fori_loop(groups * GROUP, live, one, 0)

    return finish


def fill(slab, pieces, per_piece):
    tile_size = slab.shape[2]
    kc = slab.shape[1] // 2
    for c, piece in enumerate(pieces):
        for h in range(per_piece):
            block = piece[h * tile_size : (h + 1) * tile_size, :].T
            high = block.astype(BF16)
            slab[c * per_piece + h, :kc, :] = high
            slab[c * per_piece + h, kc:, :] = (block - high.astype(F32)).astype(BF16)


def near_kernel(span, users, items, owner, meta, *refs):
    pieces = refs[:span]
    tiles = refs[span]
    sums = refs[span + 1 : -4]
    slab, buf, sems, order = refs[-4:]
    per_piece = pieces[0].shape[0] // tiles.shape[1]
    kc = sums[0].shape[1]

    def add(place, value):
        for k, part in enumerate(sums):
            part[place] += value[k * kc : (k + 1) * kc]

    finish = run_tiles(
        0, span, per_piece, users, items, owner, meta, tiles, slab, add, buf, sems, order
    )
    for part in sums:
        part[...] = jnp.zeros_like(part)
    fill(slab, pieces, per_piece)
    finish()


def far_kernel(span, orders, users, items, owner, meta, *refs):
    pieces = refs[:span]
    start, tiles = refs[span], refs[span + 1]
    outs = refs[span + 2 : -5]
    slab, buf, sems, order, acc = refs[-5:]
    tile_size = tiles.shape[1]
    per_piece = pieces[0].shape[0] // tile_size

    def add(place, value):
        acc[place] += value

    finish = run_tiles(
        span, span, per_piece, users, items, owner, meta, tiles, slab, add, buf, sems, order
    )
    acc[...] = start[...]
    fill(slab, pieces, per_piece)
    finish()
    width = tile_size // len(orders)
    for o, bits in enumerate(orders):
        cut = slice(o * width, (o + 1) * width)
        for k, place in enumerate(places(bits, 0)):
            outs[2 * o][k] = acc[place, :, cut]
        for k, place in enumerate(places(bits, 1)):
            outs[2 * o + 1][k] = acc[place, :, cut].astype(BF16)


def tile_call(kernel, scalars, pieces, extra, tiles, shapes, scratch, seconds):
    users = scalars[0].shape[0]
    tile_size = tiles.shape[1]
    blocks = len(pieces) * pieces[0].shape[0] // tile_size
    smem = pl.BlockSpec(memory_space=pltpu.SMEM)
    vmem = pl.BlockSpec(memory_space=pltpu.VMEM)
    return pl.pallas_call(
        kernel,
        out_shape=shapes,
        in_specs=[smem] * len(scalars)
        + [vmem] * (len(pieces) + len(extra))
        + [pl.BlockSpec(memory_space=pl.ANY)],
        out_specs=[vmem] * len(shapes),
        scratch_shapes=[
            pltpu.VMEM((blocks, 2 * pieces[0].shape[1], tile_size), BF16),
            pltpu.VMEM((SLOTS, tile_size, tile_size), BF16),
            pltpu.SemaphoreType.DMA((SLOTS,)),
            pltpu.SMEM((users,), jnp.int32),
        ]
        + scratch,
        compiler_params=pltpu.CompilerParams(vmem_limit_bytes=32 * 2**20),
        cost_estimate=pl.CostEstimate(
            flops=0, bytes_accessed=seconds, transcendentals=0
        ),
    )(*scalars, *pieces, *extra, tiles)


def near_sums(scalars, pieces, tiles, rows):
    tile_size = tiles.shape[1]
    kc = pieces[0].shape[1] // CHUNKS
    shapes = [jax.ShapeDtypeStruct((rows, kc, tile_size), F32)] * CHUNKS
    return tile_call(
        functools.partial(near_kernel, len(pieces)), scalars, pieces, [], tiles, shapes, [], NEAR_COST
    )


def far_sums(scalars, pieces, start, tiles, orders, cost):
    rows, kc, tile_size = start.shape
    width = tile_size // len(orders)
    shapes = []
    for _ in orders:
        shapes.append(jax.ShapeDtypeStruct((rows // 2, kc, width), F32))
        shapes.append(jax.ShapeDtypeStruct((rows // 2, kc, width), BF16))
    return tile_call(
        functools.partial(far_kernel, len(pieces), orders),
        scalars,
        pieces,
        [start],
        tiles,
        shapes,
        [pltpu.VMEM(start.shape, F32)],
        cost,
    )


def mm(a, b):
    return lax.dot_general(a, b, (((1,), (0,)), ((), ())), precision=HIGH, preferred_element_type=F32)


def mmt(a, b):
    return lax.dot_general(a, b, (((1,), (1,)), ((), ())), precision=HIGH, preferred_element_type=F32)


def factor_kernel(packed, inverse, good):
    n = packed.shape[1]
    r = lax.broadcasted_iota(jnp.int32, (n, n), 0)
    c = lax.broadcasted_iota(jnp.int32, (n, n), 1)
    mixed = packed[:n]
    flipped = mixed.T
    side = packed[n : 2 * n]
    tail = jnp.broadcast_to(packed[2 * n : 2 * n + 1], (n, n))
    first = jnp.where(r >= c, mixed, flipped)
    second = jnp.where(r < c, mixed, jnp.where(r > c, flipped, tail))
    gram = jnp.concatenate(
        [jnp.concatenate([first, side.T], axis=1), jnp.concatenate([side, second], axis=1)], axis=0
    )
    m = 2 * n
    rr = lax.broadcasted_iota(jnp.int32, (m, m), 0)
    cc = lax.broadcasted_iota(jnp.int32, (m, m), 1)
    on = rr == cc
    eye = jnp.where(on, 1.0, 0.0).astype(F32)
    low = jnp.where(rr > cc, 1.0, jnp.where(on, 0.5, 0.0)).astype(F32)
    diag = jnp.where(on, gram, 0.0)
    scale_row = lax.rsqrt(jnp.sum(diag, axis=0, keepdims=True))
    scale_col = lax.rsqrt(jnp.sum(diag, axis=1, keepdims=True))
    unit = gram * scale_row * scale_col
    off = unit - eye
    square = jnp.dot(off, off, preferred_element_type=F32)
    spread = jnp.max(jnp.sum(jnp.abs(jnp.dot(square, square, preferred_element_type=F32)), axis=1))
    w = eye - low * off
    for _ in range(NEWTON):
        err = mmt(mm(w, unit), w) - eye
        w = w - mm(low * err, w)
    last = jnp.max(jnp.sum(jnp.abs(err), axis=1))
    inflation = jnp.max(jnp.sum(w * w, axis=0))
    inverse[...] = w * scale_row
    good[0] = jnp.where((spread < 0.025) & (last < 0.01) & (inflation < 1.1), 1, 0)


def factor(packed):
    n = packed.shape[1]
    return pl.pallas_call(
        factor_kernel,
        out_shape=[jax.ShapeDtypeStruct((2 * n, 2 * n), F32), jax.ShapeDtypeStruct((1,), jnp.int32)],
        in_specs=[pl.BlockSpec(memory_space=pltpu.VMEM)],
        out_specs=[pl.BlockSpec(memory_space=pltpu.VMEM), pl.BlockSpec(memory_space=pltpu.SMEM)],
        compiler_params=pltpu.CompilerParams(vmem_limit_bytes=24 * 2**20),
        cost_estimate=pl.CostEstimate(
            flops=0, bytes_accessed=FACTOR_COST, transcendentals=0
        ),
    )(packed)


def pack(gram):
    n = gram.shape[0] // 2
    r = lax.broadcasted_iota(jnp.int32, (n, n), 0)
    c = lax.broadcasted_iota(jnp.int32, (n, n), 1)
    mixed = jnp.where(r >= c, gram[:n, :n], gram[n:, n:])
    tail = jnp.sum(jnp.where(r == c, gram[n:, n:], 0.0), axis=0, keepdims=True)
    return jnp.concatenate([mixed, gram[n:, :n], jnp.broadcast_to(tail, (8, n))], axis=0)


def full_path(rows, cols, sketch, tiles, tile_user, tile_item, tile_count, item_owner, packed):
    n = packed.shape[1]
    r = lax.broadcasted_iota(jnp.int32, (n, n), 0)
    c = lax.broadcasted_iota(jnp.int32, (n, n), 1)
    mixed, side, tail = packed[:n], packed[n : 2 * n], packed[2 * n : 2 * n + 1]
    first = jnp.where(r >= c, mixed, mixed.T)
    second = jnp.where(r < c, mixed, jnp.where(r > c, mixed.T, tail))
    gram = jnp.block([[first, side.T], [side, second]])
    lower = jnp.linalg.cholesky(gram)
    basis = lax.linalg.triangular_solve(lower, sketch, left_side=False, lower=True, transpose_a=True).astype(BF16)
    have = {0: basis}
    for bit in bits_of(cols):
        for place in list(have):
            have[place | bit] = swap(have[place], "cols", cols, bit)
    slab = jnp.concatenate([have[i] for i in range(cols)], axis=0)
    col = lax.axis_index("cols")
    row = lax.axis_index("rows")
    per_piece = sketch.shape[0] // tiles.shape[2]
    owner = item_owner[0]
    tile_size = tiles.shape[2]

    def step(index, sums):
        user = tile_user[index]
        block = lax.bitwise_xor(user // per_piece, col) * per_piece + user % per_piece
        part_rows = lax.dynamic_slice_in_dim(slab, block * tile_size, tile_size, 0)
        part = lax.dot_general(part_rows, tiles[index], (((0,), (0,)), ((), ())), preferred_element_type=F32)
        place = lax.bitwise_xor(owner[tile_item[index]], row)
        now = lax.dynamic_index_in_dim(sums, place, 0, keepdims=False)
        return lax.dynamic_update_index_in_dim(sums, now + part, place, 0)

    totals = jnp.zeros((owner.shape[0], sketch.shape[1], tile_size), F32)
    totals = lax.fori_loop(0, tile_count[0], step, totals)
    for bit in bits_of(rows):
        totals = totals[:bit] + swap(totals[bit:], "rows", rows, bit)
    return totals[0]


def after(value, *others):
    return lax.optimization_barrier((value, *others))[0]


def exchange(lanes, rows):
    got = [None] * len(lanes)
    for bit in sorted({lane[2] for lane in lanes}):
        members = [i for i, lane in enumerate(lanes) if lane[2] == bit]
        came = swap(jnp.concatenate([lanes[i][1] for i in members], axis=0), "rows", rows, 1 << bit)
        first = 0
        for i in members:
            last = first + lanes[i][1].shape[0]
            got[i] = came[first:last]
            first = last
    return got


def split(total):
    half = total.shape[0] // 2
    return total[:half], total[half:].astype(BF16)


def body(rows, cols, sketch, tiles, tile_user, tile_item, tile_count, item_owner):
    width = sketch.shape[1]
    row_bits = rows.bit_length() - 1
    first_order = tuple(range(row_bits))
    orders = (first_order, (1, 0) + first_order[2:])
    row = lax.axis_index("rows")
    col = lax.axis_index("cols")
    meta = jnp.stack([tile_count[0], row, col]).astype(jnp.int32)
    scalars = (tile_user, tile_item, item_owner[0], meta)
    kc = width // CHUNKS
    far_bit, *near_bits = bits_of(cols)

    def spread(piece):
        have = {0: piece}
        for bit in near_bits:
            for place in list(have):
                have[place | bit] = swap(have[place], "cols", cols, bit)
        return [have[i] for i in range(cols // 2)]

    fence = lax.optimization_barrier
    far = far_bit
    crossed = [swap(sketch[:, :kc], "cols", cols, far)]
    near = spread(sketch)
    crossed.append(swap(after(sketch, near[-1])[:, kc:], "cols", cols, far))
    sums = near_sums(scalars, near, tiles, rows)
    source = after(sketch, sums[0])
    gram = lax.dot_general(
        source, source, (((0,), (0,)), ((), ())), precision=HIGH, preferred_element_type=F32
    )
    packed = pack(gram)
    for bit in near_bits:
        packed = packed + swap(packed, "cols", cols, bit)
    came = swap(packed, "rows", rows, 1)
    crossed[0] = after(crossed[0], packed)
    outs = far_sums(scalars, spread(crossed[0]), sums[0], tiles, orders, EARLY_COST)
    packed, came, *outs = fence((packed, came, *outs))
    packed = packed + came
    packed = packed + swap(packed, "rows", rows, 2)
    came = swap(packed, "rows", rows, 4)
    lanes = [(outs[2 * o], outs[2 * o + 1], order[0]) for o, order in enumerate(orders)]
    got = exchange(lanes, rows)
    crossed[1] = after(crossed[1], packed)
    later = far_sums(scalars, spread(crossed[1]), sums[1], tiles, orders, LATE_COST)
    packed, came, *rest = fence((packed, came, *got, *later))
    got, later = rest[: len(got)], rest[len(got) :]
    packed = packed + came
    stages = [("cols", far)] + [("rows", 1 << b) for b in range(3, row_bits)]

    totals = [lane[0] + g.astype(F32) for lane, g in zip(lanes, got)]
    late = [(later[2 * o], later[2 * o + 1]) for o in range(len(orders))]
    done = []
    for step in range(1, row_bits + 1):
        lanes = []
        if step < row_bits:
            lanes += [(*split(t), order[step]) for t, order in zip(totals, orders)]
        lanes += [(*pair, order[step - 1]) for pair, order in zip(late, orders)]
        got = exchange(lanes, rows)
        if step <= len(stages):
            axis, bit = stages[step - 1]
            came = swap(packed, axis, rows if axis == "rows" else cols, bit)
            packed, came, *got = fence((packed, came, *got))
            packed = packed + came
        if step == len(stages) + 1:
            inverse, good = factor(after(packed, *[lane[1] for lane in lanes]))
            inverse, *got = fence((inverse, *got))
        new = [lane[0] + g.astype(F32) for lane, g in zip(lanes, got)]
        if step < row_bits:
            totals, new = new[: len(orders)], new[len(orders) :]
            late = [split(t) for t in new]
        if step >= row_bits - 1:
            done.append(jnp.concatenate([t[0] for t in (totals if step < row_bits else new)], axis=1))
    head = mm(inverse[:, :kc], done[0])
    out = lax.cond(
        good[0] > 0,
        lambda: jnp.concatenate([head[:kc], head[kc:] + mm(inverse[kc:, kc:], done[1])], axis=0),
        lambda: full_path(rows, cols, sketch, tiles, tile_user, tile_item, tile_count, item_owner, packed),
    )
    return out[None, None]


def solution(mesh):
    placed = (
        P(("rows", "cols"), None),
        P(("rows", "cols"), None, None),
        P(("rows", "cols")),
        P(("rows", "cols")),
        P(("rows", "cols")),
        P("cols", None),
    )
    return jax.shard_map(
        functools.partial(body, mesh.shape["rows"], mesh.shape["cols"]),
        mesh=mesh,
        in_specs=placed,
        out_specs=P("rows", "cols", None, None),
        check_vma=False,
    )
```

profile of v0, /device:TPU:2, one launch (start us, length us, event | category | flops | bytes accessed | tf_op | source)
XLA Modules:
  0.0 678.2 jit_solution(12397112370038127567)
XLA Ops:
  2.9 4.7 shard_map.66
  7.6 1.8 fusion.29
  11.6 3.9 collective-permute-done.9.refs_0_
  15.9 4.9 collective-permute-start.8
  20.8 4.4 shard_map.67
  25.5 4.8 collective-permute-done.11
  30.4 2.9 collective-permute-start.13
  33.3 2.1 collective-permute-start.14
  35.6 4.4 shard_map.68
  40.1 4.9 collective-permute-done.14
  47.0 9.0 %collective-permute-done.18 = bf16[6,128,256]{2,1,0:T(8,128)(2,1)S(1)} collective-permute-done((bf16[6,128,256]{2,1,0:T(8,128)(2,1)S(1)}, bf16[6,128,256]{2,1,0:T(8,128)(2,1)S(1)}, u32[]{:S(2)}, u32[]{:S(2)}) %collective-permute-start.18) | collective-permute-done | bytes 393248 | tf_op jit(solution)/shard_map/ppermute | solution.py:28
  56.5 2.4 collective-permute-start.20
  59.6 1.7 collective-permute-start.21
  61.3 3.8 shard_map.69
  67.2 6.1 collective-permute-done.23
  74.0 603.4 %conditional.1 = (f32[1,1,256,512]{3,2,1,0:T(8,128)S(1)}) conditional(s32[]{:T(128)} %bitcast.22, (s32[1]{0:T(128)}, f32[264,128]{1,0:T(8,128)S(1)}, f32[1024,256]{1,0:T(8,128)S(1)}, s32[1,8]{1,0:T(1,128)S(1)}, s32[40]{0:T(128)S(1)}, /*index=5*/s32[40]{0:T(128)S(1)}, bf16[40,512,512]{2,1,0:T(8,128)(2,1)}) %tuple.93, (f32[256,512]{1,0:T(8,128)S(1)}, ...), branch_computations={%region_1.8_spmd, %region_8.9_spmd} | conditional | flops 802537728 | bytes 78131984 | solution.py:409
  74.7 11.7 %cholesky.8 = f32[128,128]{1,0:T(8,128)S(1)} custom-call(f32[128,128]{1,0:T(8,128)S(1)} %cholesky.47), custom_call_target="Cholesky" | custom-call | tf_op jit(solution)/shard_map/cond/branch_0_fun/jit(cholesky)/cholesky | solution.py:286
  86.7 9.8 %custom-call.12 = f32[1,128,128]{1,2,0:T(8,128)S(1)} custom-call(f32[1,128,128]{2,1,0:T(8,128)S(1)} %copy.15), custom_call_target="InvertDiagBlocksLowerTriangular" | custom-call | tf_op jit(solution)/shard_map/cond/branch_0_fun/jit(cholesky)/cholesky | solution.py:286
  97.0 11.7 %cholesky.30 = f32[128,128]{1,0:T(8,128)S(1)} custom-call(f32[128,128]{1,0:T(8,128)S(1)} %convolution_subtract_fusion.1), custom_call_target="Cholesky" | custom-call | tf_op jit(solution)/shard_map/cond/branch_0_fun/jit(cholesky)/cholesky | solution.py:286
  111.0 4.0 while.13
  111.8 1.3 bitcast_dynamic-update-slice_fusion.2
  113.7 1.3 bitcast_dynamic-update-slice_fusion.2
  115.1 19.7 %custom-call.13 = f32[2,128,128]{1,2,0:T(8,128)S(1)} custom-call(f32[2,128,128]{2,1,0:T(8,128)S(1)} %get-tuple-element.262), custom_call_target="InvertDiagBlocksLowerTriangular" | custom-call | tf_op jit(solution)/shard_map/cond/branch_0_fun/triangular_solve | solution.py:287
  137.5 10.2 %collective-permute-done.1 = bf16[1024,256]{0,1:T(8,128)(2,1)S(1)} collective-permute-done((bf16[1024,256]{0,1:T(8,128)(2,1)S(1)}, bf16[1024,256]{0,1:T(8,128)(2,1)S(1)}, u32[]{:S(2)}, u32[]{:S(2)}) %collective-permute-start.1) | collective-permute-done | bytes 524320 | tf_op jit(solution)/shard_map/cond/branch_0_fun/ppermute | solution.py:28
  147.7 2.0 collective-permute-done.2
  149.7 3.1 pad_maximum_fusion
  152.8 2.5 broadcast.97
  155.3 143.2 %while.12 = (s32[]{:T(128)}, f32[8,256,512]{2,1,0:T(8,128)}, s32[]{:T(128)}, s32[40]{0:T(128)S(1)}, s32[8]{0:T(128)S(1)}, /*index=5*/s32[]{:T(128)}, s32[40]{0:T...) while((s32[]{:T(128)}, f32[8,256,512]{2,1,0:T(8,128)}, ...), condition=%wide.region_7.7_spmd, body=%wide.region_6.6_spmd.sunk | while | flops 134348832 | bytes 2884192 | solution.py:309
  163.0 1.1 constant_dynamic-slice_fusion.4
  164.1 2.1 fusion.43
  173.9 1.1 constant_dynamic-slice_fusion.4
  175.0 2.1 fusion.43
  186.0 2.2 fusion.43
  197.0 2.1 fusion.43
  207.9 2.1 fusion.43
  218.9 2.1 fusion.43
  229.8 2.1 fusion.43
  240.8 2.2 fusion.43
  251.8 2.1 fusion.43
  262.7 2.1 fusion.43
  273.7 2.2 fusion.43
  284.7 2.2 fusion.43
  295.6 2.2 fusion.43
  298.4 1.9 slice.139
  300.5 60.2 %collective-permute-done.3 = f32[4,256,512]{2,1,0:T(8,128)S(1)} collective-permute-done((f32[4,256,512]{2,1,0:T(8,128)S(1)}, f32[4,256,512]{2,1,0:T(8,128)S(1)}, u32[]{:S(2)}, u32[]{:S(2)}) %collective-permute-start.3) | collective-permute-done | bytes 2097184 | tf_op jit(solution)/shard_map/cond/branch_0_fun/ppermute | solution.py:28
  361.3 21.7 %collective-permute-done.4 = f32[2,256,512]{2,1,0:T(8,128)S(1)} collective-permute-done((f32[2,256,512]{2,1,0:T(8,128)S(1)}, f32[2,256,512]{2,1,0:T(8,128)S(1)}, u32[]{:S(2)}, u32[]{:S(2)}) %collective-permute-start.4) | collective-permute-done | bytes 1048608 | tf_op jit(solution)/shard_map/cond/branch_0_fun/ppermute | solution.py:28
  383.3 282.9 %collective-permute-start.5 = (f32[1,256,512]{2,1,0:T(8,128)S(1)}, f32[1,256,512]{2,1,0:T(8,128)S(1)}, u32[]{:S(2)}, u32[]{:S(2)}) collective-permute-start(f32[1,256,512]{2,1,0:T(8,128)S(1)} %slice.222), channel_id=1, source_target_pairs={{0,4},{4,0},{8,12},{12,8},{16,20},{20,16},{24,28},{28,24},{1,5},{5... | collective-permute-start | bytes 1572872 | tf_op jit(solution)/shard_map/cond/branch_0_fun/ppermute | solution.py:28
  666.2 10.9 %collective-permute-done.5 = f32[1,256,512]{2,1,0:T(8,128)S(1)} collective-permute-done((f32[1,256,512]{2,1,0:T(8,128)S(1)}, f32[1,256,512]{2,1,0:T(8,128)S(1)}, u32[]{:S(2)}, u32[]{:S(2)}) %collective-permute-start.5) | collective-permute-done | bytes 524320 | tf_op jit(solution)/shard_map/cond/branch_0_fun/ppermute | solution.py:28
  (173 shorter events, 55.8 us)
Async XLA Ops:
  0.0 2.9 collective-permute-start.6
  1.1 14.4 %collective-permute-start.9 = (f32[1024,128]{1,0:T(8,128)S(1)}, f32[1024,128]{1,0:T(8,128)S(1)}, u32[]{:S(2)}, u32[]{:S(2)}) collective-permute-start(f32[1024,128]{1,0:T(8,128)S(1)} %slice.180), channel_id=1, source_target_pairs={{0,2},{1,3},{2,0},{3,1},{4,6},{5,7},{6,4},{7,5},{8,10},{9,11},{10,... | collective-permute-start | bytes 1572872 | tf_op jit(solution)/shard_map/ppermute | solution.py:28
  2.9 4.7 copy-start.1
  7.6 13.2 %copy-start.3 = (s32[1,8]{1,0:T(1,128)S(1)}, s32[1,8]{1,0:T(1,128)}, u32[]{:S(2)}) copy-start(s32[1,8]{1,0:T(1,128)} %param.15) | copy-start | bytes 100
  7.6 13.2 %copy-start.4 = (s32[40]{0:T(128)S(1)}, s32[40]{0:T(128)}, u32[]{:S(2)}) copy-start(s32[40]{0:T(128)} %items.5) | copy-start | bytes 484
  7.6 13.2 %copy-start.5 = (s32[40]{0:T(128)S(1)}, s32[40]{0:T(128)}, u32[]{:S(2)}) copy-start(s32[40]{0:T(128)} %users.5) | copy-start | bytes 484
  9.5 2.1 collective-permute-start.7
  15.5 5.3 collective-permute-start.10
  15.5 14.8 %collective-permute-start.15 = (f32[1024,128]{1,0:T(8,128)S(1)}, f32[1024,128]{1,0:T(8,128)S(1)}, u32[]{:S(2)}, u32[]{:S(2)}) collective-permute-start(f32[1024,128]{1,0:T(8,128)S(1)} %slice.181), channel_id=1, source_target_pairs={{0,2},{1,3},{2,0},{3,1},{4,6},{5,7},{6,4},{7,5},{8,10},{9,11},{10,... | collective-permute-start | bytes 1572872 | tf_op jit(solution)/shard_map/ppermute | solution.py:28
  15.9 9.3 %collective-permute-start.8 = (f32[264,128]{1,0:T(8,128)S(1)}, f32[264,128]{1,0:T(8,128)S(1)}, u32[]{:S(2)}, u32[]{:S(2)}) collective-permute-start(f32[264,128]{1,0:T(8,128)S(1)} %fusion.26), channel_id=1, source_target_pairs={{0,4},{4,0},{8,12},{12,8},{16,20},{20,16},{24,28},{28,24},{1,5},{5... | collective-permute-start | bytes 405512 | tf_op jit(solution)/shard_map/ppermute | solution.py:28
  25.2 5.1 collective-permute-start.11
  30.3 5.3 collective-permute-start.16
  30.4 9.7 %collective-permute-start.13 = (bf16[4,128,256]{2,1,0:T(8,128)(2,1)S(1)}, bf16[4,128,256]{2,1,0:T(8,128)(2,1)S(1)}, u32[]{:S(2)}, u32[]{:S(2)}) collective-permute-start(bf16[4,128,256]{2,1,0:T(8,128)(2,1)S(1)} %get-tuple-element.221), channel_id=1, source_target_pairs={{0,4},{4,0},{8,12},{12,8},{16,20},{20,16},{24,28},{28,24},{1,5},{5... | collective-permute-start | bytes 786440 | tf_op jit(solution)/shard_map/ppermute | solution.py:28
  33.3 11.7 %collective-permute-start.14 = (bf16[4,128,256]{2,1,0:T(8,128)(2,1)S(1)}, bf16[4,128,256]{2,1,0:T(8,128)(2,1)S(1)}, u32[]{:S(2)}, u32[]{:S(2)}) collective-permute-start(bf16[4,128,256]{2,1,0:T(8,128)(2,1)S(1)} %get-tuple-element.222), channel_id=1, source_target_pairs={{0,8},{4,12},{8,0},{12,4},{16,24},{20,28},{24,16},{28,20},{1,9},{5... | collective-permute-start | bytes 786440 | tf_op jit(solution)/shard_map/ppermute | solution.py:28
  35.4 9.6 %collective-permute-start.12 = (f32[264,128]{1,0:T(8,128)S(1)}, f32[264,128]{1,0:T(8,128)S(1)}, u32[]{:S(2)}, u32[]{:S(2)}) collective-permute-start(f32[264,128]{1,0:T(8,128)S(1)} %add.145), channel_id=1, source_target_pairs={{0,16},{4,20},{8,24},{12,28},{16,0},{20,4},{24,8},{28,12},{1,17},{... | collective-permute-start | bytes 405512 | tf_op jit(solution)/shard_map/ppermute | solution.py:28
  45.2 10.8 %collective-permute-start.18 = (bf16[6,128,256]{2,1,0:T(8,128)(2,1)S(1)}, bf16[6,128,256]{2,1,0:T(8,128)(2,1)S(1)}, u32[]{:S(2)}, u32[]{:S(2)}) collective-permute-start(bf16[6,128,256]{2,1,0:T(8,128)(2,1)S(1)} %pad_maximum_fusion.2), channel_id=1, source_target_pairs={{0,8},{4,12},{8,0},{12,4},{16,24},{20,28},{24,16},{28,20},{1,9},{5... | collective-permute-start | bytes 1179656 | tf_op jit(solution)/shard_map/ppermute | solution.py:28
  45.7 10.5 %collective-permute-start.19 = (bf16[6,128,256]{2,1,0:T(8,128)(2,1)S(1)}, bf16[6,128,256]{2,1,0:T(8,128)(2,1)S(1)}, u32[]{:S(2)}, u32[]{:S(2)}) collective-permute-start(bf16[6,128,256]{2,1,0:T(8,128)(2,1)S(1)} %pad_maximum_fusion.3), channel_id=1, source_target_pairs={{0,4},{4,0},{8,12},{12,8},{16,20},{20,16},{24,28},{28,24},{1,5},{5... | collective-permute-start | bytes 1179656 | tf_op jit(solution)/shard_map/ppermute | solution.py:28
  46.3 9.9 %collective-permute-start.17 = (f32[264,128]{1,0:T(8,128)S(1)}, f32[264,128]{1,0:T(8,128)S(1)}, u32[]{:S(2)}, u32[]{:S(2)}) collective-permute-start(f32[264,128]{1,0:T(8,128)S(1)} %add.146), channel_id=1, source_target_pairs={{0,2},{1,3},{2,0},{3,1},{4,6},{5,7},{6,4},{7,5},{8,10},{9,11},{10,... | collective-permute-start | bytes 405512 | tf_op jit(solution)/shard_map/ppermute | solution.py:28
  56.5 9.4 %collective-permute-start.20 = (bf16[2,128,256]{2,1,0:T(8,128)(2,1)S(1)}, bf16[2,128,256]{2,1,0:T(8,128)(2,1)S(1)}, u32[]{:S(2)}, u32[]{:S(2)}) collective-permute-start(bf16[2,128,256]{2,1,0:T(8,128)(2,1)S(1)} %pad_maximum_fusion.6), channel_id=1, source_target_pairs={{0,16},{4,20},{8,24},{12,28},{16,0},{20,4},{24,8},{28,12},{1,17},{... | collective-permute-start | bytes 393224 | tf_op jit(solution)/shard_map/ppermute | solution.py:28
  58.9 6.9 %collective-permute-start.22 = (bf16[2,128,256]{2,1,0:T(8,128)(2,1)S(1)}, bf16[2,128,256]{2,1,0:T(8,128)(2,1)S(1)}, u32[]{:S(2)}, u32[]{:S(2)}) collective-permute-start(bf16[2,128,256]{2,1,0:T(8,128)(2,1)S(1)} %slice.293), channel_id=1, source_target_pairs={{0,4},{4,0},{8,12},{12,8},{16,20},{20,16},{24,28},{28,24},{1,5},{5... | collective-permute-start | bytes 393224 | tf_op jit(solution)/shard_map/ppermute | solution.py:28
  59.6 6.2 collective-permute-start.21
  66.0 7.2 %collective-permute-start.23 = (bf16[2,128,256]{2,1,0:T(8,128)(2,1)S(1)}, bf16[2,128,256]{2,1,0:T(8,128)(2,1)S(1)}, u32[]{:S(2)}, u32[]{:S(2)}) collective-permute-start(bf16[2,128,256]{2,1,0:T(8,128)(2,1)S(1)} %pad_maximum_fusion.7), channel_id=1, source_target_pairs={{0,16},{4,20},{8,24},{12,28},{16,0},{20,4},{24,8},{28,12},{1,17},{... | collective-permute-start | bytes 393224 | tf_op jit(solution)/shard_map/ppermute | solution.py:28
  137.1 10.6 %collective-permute-start.1 = (bf16[1024,256]{0,1:T(8,128)(2,1)S(1)}, bf16[1024,256]{0,1:T(8,128)(2,1)S(1)}, u32[]{:S(2)}, u32[]{:S(2)}) collective-permute-start(bf16[1024,256]{0,1:T(8,128)(2,1)S(1)} %pad_maximum_fusion.1), channel_id=1, source_target_pairs={{0,2},{1,3},{2,0},{3,1},{4,6},{5,7},{6,4},{7,5},{8,10},{9,11},{10,... | collective-permute-start | bytes 1572872 | tf_op jit(solution)/shard_map/cond/branch_0_fun/ppermute | solution.py:28
  137.5 10.2 %collective-permute-start = (bf16[1024,256]{0,1:T(8,128)(2,1)S(1)}, bf16[1024,256]{0,1:T(8,128)(2,1)}, u32[]{:S(2)}, u32[]{:S(2)}) collective-permute-start(bf16[1024,256]{0,1:T(8,128)(2,1)S(1)} %pad_maximum_fusion.1), channel_id=1, source_target_pairs={{0,1},{1,0},{2,3},{3,2},{4,5},{5,4},{6,7},{7,6},{8,9},{9,8},{10,11... | collective-permute-start | bytes 1572872 | tf_op jit(solution)/shard_map/cond/branch_0_fun/ppermute | solution.py:28
  147.7 2.0 collective-permute-start.2
  298.4 62.2 %copy-start = (f32[8,256,512]{2,1,0:T(8,128)S(1)}, f32[8,256,512]{2,1,0:T(8,128)}, u32[]{:S(2)}) copy-start(f32[8,256,512]{2,1,0:T(8,128)} %get-tuple-element.166) | copy-start | bytes 12582916 | tf_op jit(solution)/shard_map/cond
  300.4 60.3 %collective-permute-start.3 = (f32[4,256,512]{2,1,0:T(8,128)S(1)}, f32[4,256,512]{2,1,0:T(8,128)S(1)}, u32[]{:S(2)}, u32[]{:S(2)}) collective-permute-start(f32[4,256,512]{2,1,0:T(8,128)S(1)} %slice.139), channel_id=1, source_target_pairs={{0,16},{4,20},{8,24},{12,28},{16,0},{20,4},{24,8},{28,12},{1,17},{... | collective-permute-start | bytes 6291464 | tf_op jit(solution)/shard_map/cond/branch_0_fun/ppermute | solution.py:28
  361.2 21.8 %collective-permute-start.4 = (f32[2,256,512]{2,1,0:T(8,128)S(1)}, f32[2,256,512]{2,1,0:T(8,128)S(1)}, u32[]{:S(2)}, u32[]{:S(2)}) collective-permute-start(f32[2,256,512]{2,1,0:T(8,128)S(1)} %slice.220), channel_id=1, source_target_pairs={{0,8},{4,12},{8,0},{12,4},{16,24},{20,28},{24,16},{28,20},{1,9},{5... | collective-permute-start | bytes 3145736 | tf_op jit(solution)/shard_map/cond/branch_0_fun/ppermute | solution.py:28
  383.3 293.8 %collective-permute-start.5 = (f32[1,256,512]{2,1,0:T(8,128)S(1)}, f32[1,256,512]{2,1,0:T(8,128)S(1)}, u32[]{:S(2)}, u32[]{:S(2)}) collective-permute-start(f32[1,256,512]{2,1,0:T(8,128)S(1)} %slice.222), channel_id=1, source_target_pairs={{0,4},{4,0},{8,12},{12,8},{16,20},{20,16},{24,28},{28,24},{1,5},{5... | collective-permute-start | bytes 1572872 | tf_op jit(solution)/shard_map/cond/branch_0_fun/ppermute | solution.py:28
  677.4 0.8 copy-start.2
where the time goes:
time: 691 us; the launch traced here: 678 us
  starting transfers between devices  302 us (44%)
  waiting for transfers between devices  136 us (20%)
  loops' own time  77.8 us (11%)
  other arithmetic  59.4 us (9%)
  local copies, waits for them, and re-layouts  50.7 us (7%)
  matrix products  33.1 us (5%)
  Pallas kernels  17.3 us (3%)
    ppermute x24, starting transfers between devices, swap(): return lax.ppermute(x, axis, [(i, i ^ bit) for i in range(count)])  302 us
    ppermute x24, waiting for transfers between devices, swap(): return lax.ppermute(x, axis, [(i, i ^ bit) for i in range(count)])  136 us
    another operation x1, loops' own time, full_path(): totals = lax.fori_loop(0, tile_count[0], step, totals)  75.8 us
    another operation x6, other arithmetic, full_path(): lower = jnp.linalg.cholesky(gram)  34.2 us
    dot_general x13, matrix products, step(): lax.dot_general(part_rows, tiles[index], (((0,), (0,)), ((), ())), prefer...  27.9 us
    another operation x5, other arithmetic, full_path(): lax.linalg.triangular_solve(lower, sketch, left_side=False, lower=True, t...  19.8 us
    dynamic_slice x26, local copies, waits for them, and re-layouts, step(): place = lax.bitwise_xor(owner[tile_item[index]], row)  16.9 us
    dynamic_slice x13, local copies, waits for them, and re-layouts, step(): now = lax.dynamic_index_in_dim(sums, place, 0, keepdims=False)  14.1 us
  transfers between devices with their start and end apart: 24, of which 13 were waited for; matrix products, arithmetic and copies ran while one was open for 1% of the time, Pallas kernels for 3%

commit v1 on v0

--- a/solution.py
+++ b/solution.py
@@ -11,12 +11,13 @@
 BF16 = jnp.bfloat16
 HIGH = lax.Precision.HIGHEST
 SLOTS = 12
+SPARE = 4 * 2**20
 GROUP = 4
 NEAR_COST = 200 * 2**20
 EARLY_COST = 1024
 LATE_COST = 1024
 FACTOR_COST = 200 * 2**20
-CHUNKS = 2
+CHUNKS = (160, 96)
 NEWTON = 2
 
 
@@ -69,8 +70,7 @@
                 buf[lax.rem(first + q, SLOTS)],
                 preferred_element_type=F32,
             )
-            half = both.shape[0] // 2
-            found.append(both[:half] + both[half:])
+            found.append(both)
         for q in range(size):
             add(lax.bitwise_xor(owner[items[order[first + q]]], row), found[q])
         for q in range(size):
@@ -95,15 +95,37 @@
     return finish
 
 
+def split_kernel(sketch, whole, *chunks):
+    flat = sketch[...].T
+    high = flat.astype(BF16)
+    low = (flat - high.astype(F32)).astype(BF16)
+    first = 0
+    for chunk in chunks:
+        kc = chunk.shape[0] // 2
+        for i, part in enumerate((high, low)):
+            rows = part[first : first + kc]
+            chunk[i * kc : (i + 1) * kc, :] = rows
+            whole[2 * first + i * kc : 2 * first + (i + 1) * kc, :] = rows
+        first += kc
+
+
+def split_sketch(sketch):
+    users, width = sketch.shape
+    vmem = pl.BlockSpec(memory_space=pltpu.VMEM)
+    return pl.pallas_call(
+        split_kernel,
+        out_shape=[jax.ShapeDtypeStruct((2 * k, users), BF16) for k in (width, *CHUNKS)],
+        in_specs=[vmem],
+        out_specs=[vmem] * (1 + len(CHUNKS)),
+        compiler_params=pltpu.CompilerParams(vmem_limit_bytes=16 * 2**20),
+    )(sketch)
+
+
 def fill(slab, pieces, per_piece):
     tile_size = slab.shape[2]
-    kc = slab.shape[1] // 2
     for c, piece in enumerate(pieces):
         for h in range(per_piece):
-            block = piece[h * tile_size : (h + 1) * tile_size, :].T
-            high = block.astype(BF16)
-            slab[c * per_piece + h, :kc, :] = high
-            slab[c * per_piece + h, kc:, :] = (block - high.astype(F32)).astype(BF16)
+            slab[c * per_piece + h] = piece[:, h * tile_size : (h + 1) * tile_size]
 
 
 def near_kernel(span, users, items, owner, meta, *refs):
@@ -111,12 +133,14 @@
     tiles = refs[span]
     sums = refs[span + 1 : -4]
     slab, buf, sems, order = refs[-4:]
-    per_piece = pieces[0].shape[0] // tiles.shape[1]
-    kc = sums[0].shape[1]
-
-    def add(place, value):
-        for k, part in enumerate(sums):
-            part[place] += value[k * kc : (k + 1) * kc]
+    per_piece = pieces[0].shape[1] // tiles.shape[1]
+
+    def add(place, both):
+        first = 0
+        for part in sums:
+            kc = part.shape[1]
+            part[place] += both[first : first + kc] + both[first + kc : first + 2 * kc]
+            first += 2 * kc
 
     finish = run_tiles(
         0, span, per_piece, users, items, owner, meta, tiles, slab, add, buf, sems, order
@@ -133,10 +157,11 @@
     outs = refs[span + 2 : -5]
     slab, buf, sems, order, acc = refs[-5:]
     tile_size = tiles.shape[1]
-    per_piece = pieces[0].shape[0] // tile_size
-
-    def add(place, value):
-        acc[place] += value
+    per_piece = pieces[0].shape[1] // tile_size
+    kc = pieces[0].shape[0] // 2
+
+    def add(place, both):
+        acc[place] += both[:kc] + both[kc:]
 
     finish = run_tiles(
         span, span, per_piece, users, items, owner, meta, tiles, slab, add, buf, sems, order
@@ -153,12 +178,15 @@
             outs[2 * o + 1][k] = acc[place, :, cut].astype(BF16)
 
 
-def tile_call(kernel, scalars, pieces, extra, tiles, shapes, scratch, seconds):
+def tile_call(kernel, scalars, pieces, extra, tiles, shapes, scratch, cost):
     users = scalars[0].shape[0]
     tile_size = tiles.shape[1]
-    blocks = len(pieces) * pieces[0].shape[0] // tile_size
+    blocks = len(pieces) * pieces[0].shape[1] // tile_size
     smem = pl.BlockSpec(memory_space=pltpu.SMEM)
     vmem = pl.BlockSpec(memory_space=pltpu.VMEM)
+    slab = jax.ShapeDtypeStruct((blocks, pieces[0].shape[0], tile_size), BF16)
+    buf = jax.ShapeDtypeStruct((SLOTS, tile_size, tile_size), BF16)
+    held = sum(x.size * x.dtype.itemsize for x in (*pieces, *extra, *shapes, *scratch, slab, buf))
     return pl.pallas_call(
         kernel,
         out_shape=shapes,
@@ -167,23 +195,20 @@
         + [pl.BlockSpec(memory_space=pl.ANY)],
         out_specs=[vmem] * len(shapes),
         scratch_shapes=[
-            pltpu.VMEM((blocks, 2 * pieces[0].shape[1], tile_size), BF16),
-            pltpu.VMEM((SLOTS, tile_size, tile_size), BF16),
+            pltpu.VMEM(slab.shape, BF16),
+            pltpu.VMEM(buf.shape, BF16),
             pltpu.SemaphoreType.DMA((SLOTS,)),
             pltpu.SMEM((users,), jnp.int32),
         ]
-        + scratch,
-        compiler_params=pltpu.CompilerParams(vmem_limit_bytes=32 * 2**20),
-        cost_estimate=pl.CostEstimate(
-            flops=0, bytes_accessed=seconds, transcendentals=0
-        ),
+        + [pltpu.VMEM(x.shape, x.dtype) for x in scratch],
+        compiler_params=pltpu.CompilerParams(vmem_limit_bytes=held + SPARE),
+        cost_estimate=pl.CostEstimate(flops=0, bytes_accessed=cost, transcendentals=0),
     )(*scalars, *pieces, *extra, tiles)
 
 
 def near_sums(scalars, pieces, tiles, rows):
     tile_size = tiles.shape[1]
-    kc = pieces[0].shape[1] // CHUNKS
-    shapes = [jax.ShapeDtypeStruct((rows, kc, tile_size), F32)] * CHUNKS
+    shapes = [jax.ShapeDtypeStruct((rows, kc, tile_size), F32) for kc in CHUNKS]
     return tile_call(
         functools.partial(near_kernel, len(pieces)), scalars, pieces, [], tiles, shapes, [], NEAR_COST
     )
@@ -203,7 +228,7 @@
         [start],
         tiles,
         shapes,
-        [pltpu.VMEM(start.shape, F32)],
+        [jax.ShapeDtypeStruct(start.shape, F32)],
         cost,
     )
 
@@ -266,6 +291,29 @@
     )(packed)
 
 
+def last_kernel(inverse, early, keep0, keep1, came, out):
+    left = keep0[0] + came[0].astype(F32)
+    right = keep1[0] + came[1].astype(F32)
+    total = jnp.concatenate([early[...], jnp.concatenate([left, right], axis=1)], axis=0)
+    w = inverse[...]
+    wh, th = w.astype(BF16), total.astype(BF16)
+    wl = (w - wh.astype(F32)).astype(BF16)
+    tl = (total - th.astype(F32)).astype(BF16)
+    small = jnp.dot(wh, tl, preferred_element_type=F32) + jnp.dot(wl, th, preferred_element_type=F32)
+    out[...] = jnp.dot(wh, th, preferred_element_type=F32) + small
+
+
+def last(inverse, early, keeps, came):
+    vmem = pl.BlockSpec(memory_space=pltpu.VMEM)
+    return pl.pallas_call(
+        last_kernel,
+        out_shape=jax.ShapeDtypeStruct((inverse.shape[0], early.shape[1]), F32),
+        in_specs=[vmem] * 5,
+        out_specs=vmem,
+        compiler_params=pltpu.CompilerParams(vmem_limit_bytes=16 * 2**20),
+    )(inverse, early, *keeps, came)
+
+
 def pack(gram):
     n = gram.shape[0] // 2
     r = lax.broadcasted_iota(jnp.int32, (n, n), 0)
@@ -317,16 +365,24 @@
 
 
 def exchange(lanes, rows):
-    got = [None] * len(lanes)
+    groups = []
     for bit in sorted({lane[2] for lane in lanes}):
         members = [i for i, lane in enumerate(lanes) if lane[2] == bit]
-        came = swap(jnp.concatenate([lanes[i][1] for i in members], axis=0), "rows", rows, 1 << bit)
+        sent = [lanes[i][1].reshape(-1, lanes[i][1].shape[2]) for i in members]
+        groups.append((members, swap(jnp.concatenate(sent, axis=0), "rows", rows, 1 << bit)))
+    return groups
+
+
+def received(lanes, groups):
+    got = [None] * len(lanes)
+    for members, came in groups:
         first = 0
         for i in members:
-            last = first + lanes[i][1].shape[0]
-            got[i] = came[first:last]
-            first = last
-    return got
+            shape = lanes[i][1].shape
+            size = shape[0] * shape[1]
+            got[i] = came[first : first + size].reshape(shape)
+            first += size
+    return [lane[0] + g.astype(F32) for lane, g in zip(lanes, got)]
 
 
 def split(total):
@@ -335,7 +391,6 @@
 
 
 def body(rows, cols, sketch, tiles, tile_user, tile_item, tile_count, item_owner):
-    width = sketch.shape[1]
     row_bits = rows.bit_length() - 1
     first_order = tuple(range(row_bits))
     orders = (first_order, (1, 0) + first_order[2:])
@@ -343,7 +398,6 @@
     col = lax.axis_index("cols")
     meta = jnp.stack([tile_count[0], row, col]).astype(jnp.int32)
     scalars = (tile_user, tile_item, item_owner[0], meta)
-    kc = width // CHUNKS
     far_bit, *near_bits = bits_of(cols)
 
     def spread(piece):
@@ -355,60 +409,66 @@
 
     fence = lax.optimization_barrier
     far = far_bit
-    crossed = [swap(sketch[:, :kc], "cols", cols, far)]
-    near = spread(sketch)
-    crossed.append(swap(after(sketch, near[-1])[:, kc:], "cols", cols, far))
-    sums = near_sums(scalars, near, tiles, rows)
-    source = after(sketch, sums[0])
+    whole, *chunks = split_sketch(sketch)
+    near = spread(whole)
+    crossed = [swap(chunk, "cols", cols, far) for chunk in chunks]
     gram = lax.dot_general(
-        source, source, (((0,), (0,)), ((), ())), precision=HIGH, preferred_element_type=F32
+        sketch, sketch, (((0,), (0,)), ((), ())), precision=HIGH, preferred_element_type=F32
     )
     packed = pack(gram)
     for bit in near_bits:
         packed = packed + swap(packed, "cols", cols, bit)
     came = swap(packed, "rows", rows, 1)
+    near[0] = after(near[0], packed)
+    sums = near_sums(scalars, near, tiles, rows)
+    packed, came, *sums = fence((packed, came, *sums))
+    packed = packed + came
+    came = swap(packed, "rows", rows, 2)
     crossed[0] = after(crossed[0], packed)
     outs = far_sums(scalars, spread(crossed[0]), sums[0], tiles, orders, EARLY_COST)
     packed, came, *outs = fence((packed, came, *outs))
     packed = packed + came
-    packed = packed + swap(packed, "rows", rows, 2)
     came = swap(packed, "rows", rows, 4)
     lanes = [(outs[2 * o], outs[2 * o + 1], order[0]) for o, order in enumerate(orders)]
-    got = exchange(lanes, rows)
+    groups = exchange(lanes, rows)
     crossed[1] = after(crossed[1], packed)
     later = far_sums(scalars, spread(crossed[1]), sums[1], tiles, orders, LATE_COST)
-    packed, came, *rest = fence((packed, came, *got, *later))
-    got, later = rest[: len(got)], rest[len(got) :]
+    flying = [g[1] for g in groups]
+    packed, came, *rest = fence((packed, came, *flying, *later))
+    groups = [(g[0], x) for g, x in zip(groups, rest)]
+    later = rest[len(groups) :]
     packed = packed + came
     stages = [("cols", far)] + [("rows", 1 << b) for b in range(3, row_bits)]
 
-    totals = [lane[0] + g.astype(F32) for lane, g in zip(lanes, got)]
+    totals = received(lanes, groups)
     late = [(later[2 * o], later[2 * o + 1]) for o in range(len(orders))]
-    done = []
     for step in range(1, row_bits + 1):
         lanes = []
         if step < row_bits:
             lanes += [(*split(t), order[step]) for t, order in zip(totals, orders)]
         lanes += [(*pair, order[step - 1]) for pair, order in zip(late, orders)]
-        got = exchange(lanes, rows)
+        groups = exchange(lanes, rows)
+        flying = [g[1] for g in groups]
         if step <= len(stages):
             axis, bit = stages[step - 1]
             came = swap(packed, axis, rows if axis == "rows" else cols, bit)
-            packed, came, *got = fence((packed, came, *got))
+            packed, came, *flying = fence((packed, came, *flying))
             packed = packed + came
         if step == len(stages) + 1:
             inverse, good = factor(after(packed, *[lane[1] for lane in lanes]))
-            inverse, *got = fence((inverse, *got))
-        new = [lane[0] + g.astype(F32) for lane, g in zip(lanes, got)]
+            inverse, *flying = fence((inverse, *flying))
+        groups = [(g[0], x) for g, x in zip(groups, flying)]
         if step < row_bits:
+            new = received(lanes, groups)
             totals, new = new[: len(orders)], new[len(orders) :]
             late = [split(t) for t in new]
-        if step >= row_bits - 1:
-            done.append(jnp.concatenate([t[0] for t in (totals if step < row_bits else new)], axis=1))
-    head = mm(inverse[:, :kc], done[0])
+        if step == row_bits - 1:
+            early = jnp.concatenate([t[0] for t in totals], axis=1)
+    keeps = [lane[0] for lane in lanes]
+    came = groups[0][1].reshape(len(lanes), *lanes[0][1].shape[1:])
     out = lax.cond(
         good[0] > 0,
-        lambda: jnp.concatenate([head[:kc], head[kc:] + mm(inverse[kc:, kc:], done[1])], axis=0),
+        lambda: last(inverse, early, keeps, came),
         lambda: full_path(rows, cols, sketch, tiles, tile_user, tile_item, tile_count, item_owner, packed),
     )
     return out[None, None]

time: 691 us -> 682 us (0.987)
  starting transfers between devices: 302 us -> 321 us
  waiting for transfers between devices: 136 us -> 127 us
    ppermute x24, starting transfers between devices: 302 us -> 321 us  [swap(): return lax.ppermute(x, axis, [(i, i ^ bit) for i in range(count)])]
    ppermute x24, waiting for transfers between devices: 136 us -> 127 us  [swap(): return lax.ppermute(x, axis, [(i, i ^ bit) for i in range(count)])]
    dot_general x13 -> x11, matrix products: 27.9 us -> 23.7 us  [step(): lax.dot_general(part_rows, tiles[index], (((0,), (0,)), ((), ())), prefer...]
    dynamic_slice x26 -> x22, local copies, waits for them, and re-layouts: 16.9 us -> 14.6 us  [step(): place = lax.bitwise_xor(owner[tile_item[index]], row)]
    dynamic_slice x13 -> x11, local copies, waits for them, and re-layouts: 14.1 us -> 11.9 us  [step(): now = lax.dynamic_index_in_dim(sums, place, 0, keepdims=False)]
  transfers between devices with their start and end apart: 24 -> 24, of which waited for: 13 -> 15; matrix products, arithmetic and copies ran while one was open for 1% -> 1% of each run, Pallas kernels for 3% -> 2%
where the time goes in v1:
time: 682 us; the launch traced here: 672 us
  starting transfers between devices  321 us (47%)
  waiting for transfers between devices  127 us (19%)
  loops' own time  71.4 us (10%)
  other arithmetic  59.5 us (9%)
  local copies, waits for them, and re-layouts  44.9 us (7%)
  matrix products  29.7 us (4%)
  Pallas kernels  17 us (2%)
    ppermute x24, starting transfers between devices, swap(): return lax.ppermute(x, axis, [(i, i ^ bit) for i in range(count)])  321 us
    ppermute x24, waiting for transfers between devices, swap(): return lax.ppermute(x, axis, [(i, i ^ bit) for i in range(count)])  127 us
    another operation x1, loops' own time, full_path(): totals = lax.fori_loop(0, tile_count[0], step, totals)  69.3 us
    another operation x6, other arithmetic, full_path(): lower = jnp.linalg.cholesky(gram)  34.2 us
    dot_general x11, matrix products, step(): lax.dot_general(part_rows, tiles[index], (((0,), (0,)), ((), ())), prefer...  23.7 us
    another operation x5, other arithmetic, full_path(): lax.linalg.triangular_solve(lower, sketch, left_side=False, lower=True, t...  19.8 us
    dynamic_slice x22, local copies, waits for them, and re-layouts, step(): place = lax.bitwise_xor(owner[tile_item[index]], row)  14.6 us
  transfers between devices with their start and end apart: 24, of which 15 were waited for; matrix products, arithmetic and copies ran while one was open for 1% of the time, Pallas kernels for 2%

profile of v1, /device:TPU:2, one launch (start us, length us, event | category | flops | bytes accessed | tf_op | source)
XLA Modules:
  0.0 672.3 jit_solution(6511634843462004636)
XLA Ops:
  0.0 1.7 shard_map.66
  2.5 3.4 fusion.21
  7.5 2.1 collective-permute-start.7
  10.4 4.9 shard_map.67
  16.3 2.7 collective-permute-done.10.refs_0_
  19.3 2.4 collective-permute-start.9
  21.7 3.4 shard_map.68
  25.6 4.9 collective-permute-done.15.refs_0_
  30.5 1.5 collective-permute-start.13
  32.0 1.6 collective-permute-start.14
  33.6 4.1 collective-permute-start.12
  37.7 3.0 shard_map.69
  40.7 3.1 collective-permute-done.12
  45.6 5.5 collective-permute-start.19
  51.5 4.7 collective-permute-done.17
  56.3 2.9 collective-permute-done.19
  60.0 1.6 collective-permute-start.22
  61.7 1.8 collective-permute-start.21
  63.5 3.9 shard_map.70
  69.8 6.3 collective-permute-done.23
  76.0 595.5 %conditional.1 = (f32[1,1,256,512]{3,2,1,0:T(8,128)S(1)}) conditional(s32[]{:T(128)} %bitcast.35, (s32[1]{0:T(128)}, f32[264,128]{1,0:T(8,128)S(1)}, f32[1024,256]{1,0:T(8,128)S(1)}, s32[1,8]{1,0:T(1,128)S(1)}, s32[40]{0:T(128)S(1)}, /*index=5*/s32[40]{0:T(128)S(1)}, bf16[40,512,512]{2,1,0:T(8,128)(2,1)}) %tuple.92, (f32[2,96,256]{2,1,0:T(8,128)S(1)}, ...), branch_computations={%region_1.8_spmd, %region_8.9_spmd} | conditional | flops 802537728 | bytes 78131984 | solution.py:469
  76.7 11.7 %cholesky.8 = f32[128,128]{1,0:T(8,128)S(1)} custom-call(f32[128,128]{1,0:T(8,128)S(1)} %cholesky.47), custom_call_target="Cholesky" | custom-call | tf_op jit(solution)/shard_map/cond/branch_0_fun/jit(cholesky)/cholesky | solution.py:334
  88.7 9.8 %custom-call.12 = f32[1,128,128]{1,2,0:T(8,128)S(1)} custom-call(f32[1,128,128]{2,1,0:T(8,128)S(1)} %copy.15), custom_call_target="InvertDiagBlocksLowerTriangular" | custom-call | tf_op jit(solution)/shard_map/cond/branch_0_fun/jit(cholesky)/cholesky | solution.py:334
  99.1 11.7 %cholesky.30 = f32[128,128]{1,0:T(8,128)S(1)} custom-call(f32[128,128]{1,0:T(8,128)S(1)} %convolution_subtract_fusion.1), custom_call_target="Cholesky" | custom-call | tf_op jit(solution)/shard_map/cond/branch_0_fun/jit(cholesky)/cholesky | solution.py:334
  113.1 4.2 while.13
  113.9 1.3 bitcast_dynamic-update-slice_fusion.2
  117.3 19.7 %custom-call.13 = f32[2,128,128]{1,2,0:T(8,128)S(1)} custom-call(f32[2,128,128]{2,1,0:T(8,128)S(1)} %get-tuple-element.277), custom_call_target="InvertDiagBlocksLowerTriangular" | custom-call | tf_op jit(solution)/shard_map/cond/branch_0_fun/triangular_solve | solution.py:335
  139.7 13.2 %collective-permute-done.1 = bf16[1024,256]{0,1:T(8,128)(2,1)S(1)} collective-permute-done((bf16[1024,256]{0,1:T(8,128)(2,1)S(1)}, bf16[1024,256]{0,1:T(8,128)(2,1)S(1)}, u32[]{:S(2)}, u32[]{:S(2)}) %collective-permute-start.1) | collective-permute-done | bytes 524320 | tf_op jit(solution)/shard_map/cond/branch_0_fun/ppermute | solution.py:29
  152.8 2.0 collective-permute-done.2
  154.9 3.1 pad_maximum_fusion
  157.9 2.5 broadcast.97
  160.4 126.9 %while.12 = (s32[]{:T(128)}, f32[8,256,512]{2,1,0:T(8,128)}, s32[]{:T(128)}, s32[40]{0:T(128)S(1)}, s32[8]{0:T(128)S(1)}, /*index=5*/s32[]{:T(128)}, s32[40]{0:T...) while((s32[]{:T(128)}, f32[8,256,512]{2,1,0:T(8,128)}, ...), condition=%wide.region_7.7_spmd, body=%wide.region_6.6_spmd.sunk | while | flops 134348832 | bytes 2884192 | solution.py:357
  169.7 2.1 fusion.34
  181.2 2.2 fusion.34
  192.7 2.1 fusion.34
  204.2 2.2 fusion.34
  215.7 2.2 fusion.34
  227.2 2.1 fusion.34
  238.6 2.2 fusion.34
  250.1 2.2 fusion.34
  261.6 2.1 fusion.34
  273.1 2.1 fusion.34
  284.5 2.1 fusion.34
  287.3 1.9 slice.125
  289.3 61.1 %collective-permute-done.3 = f32[4,256,512]{2,1,0:T(8,128)S(1)} collective-permute-done((f32[4,256,512]{2,1,0:T(8,128)S(1)}, f32[4,256,512]{2,1,0:T(8,128)S(1)}, u32[]{:S(2)}, u32[]{:S(2)}) %collective-permute-start.3) | collective-permute-done | bytes 2097184 | tf_op jit(solution)/shard_map/cond/branch_0_fun/ppermute | solution.py:29
  351.0 297.6 %collective-permute-start.4 = (f32[2,256,512]{2,1,0:T(8,128)S(1)}, f32[2,256,512]{2,1,0:T(8,128)S(1)}, u32[]{:S(2)}, u32[]{:S(2)}) collective-permute-start(f32[2,256,512]{2,1,0:T(8,128)S(1)} %slice.191), channel_id=1, source_target_pairs={{0,8},{4,12},{8,0},{12,4},{16,24},{20,28},{24,16},{28,20},{1,9},{5... | collective-permute-start | bytes 3145736 | tf_op jit(solution)/shard_map/cond/branch_0_fun/ppermute | solution.py:29
  648.7 12.8 %collective-permute-done.4 = f32[2,256,512]{2,1,0:T(8,128)S(1)} collective-permute-done((f32[2,256,512]{2,1,0:T(8,128)S(1)}, f32[2,256,512]{2,1,0:T(8,128)S(1)}, u32[]{:S(2)}, u32[]{:S(2)}) %collective-permute-start.4) | collective-permute-done | bytes 1048608 | tf_op jit(solution)/shard_map/cond/branch_0_fun/ppermute | solution.py:29
  661.8 9.4 %collective-permute-done.5 = f32[1,256,512]{2,1,0:T(8,128)S(1)} collective-permute-done((f32[1,256,512]{2,1,0:T(8,128)S(1)}, f32[1,256,512]{2,1,0:T(8,128)S(1)}, u32[]{:S(2)}, u32[]{:S(2)}) %collective-permute-start.5) | collective-permute-done | bytes 524320 | tf_op jit(solution)/shard_map/cond/branch_0_fun/ppermute | solution.py:29
  (162 shorter events, 52.2 us)
Async XLA Ops:
  0.0 10.4 %copy-start.6 = (s32[40]{0:T(128)S(1)}, s32[40]{0:T(128)}, u32[]{:S(2)}) copy-start(s32[40]{0:T(128)} %items.5) | copy-start | bytes 484
  0.0 10.4 %copy-start.7 = (s32[40]{0:T(128)S(1)}, s32[40]{0:T(128)}, u32[]{:S(2)}) copy-start(s32[40]{0:T(128)} %users.5) | copy-start | bytes 484
  0.0 10.4 %copy-start.5 = (s32[1,8]{1,0:T(1,128)S(1)}, s32[1,8]{1,0:T(1,128)}, u32[]{:S(2)}) copy-start(s32[1,8]{1,0:T(1,128)} %param.15) | copy-start | bytes 100
  1.7 0.8 copy-start
  2.5 16.5 %collective-permute-start.10 = (bf16[320,1024]{1,0:T(8,128)(2,1)S(1)}, bf16[320,1024]{1,0:T(8,128)(2,1)S(1)}, u32[]{:S(2)}, u32[]{:S(2)}) collective-permute-start(bf16[320,1024]{1,0:T(8,128)(2,1)S(1)} %get-tuple-element.230), channel_id=1, source_target_pairs={{0,2},{1,3},{2,0},{3,1},{4,6},{5,7},{6,4},{7,5},{8,10},{9,11},{10,... | collective-permute-start | bytes 1966088 | tf_op jit(solution)/shard_map/ppermute | solution.py:29
  2.5 7.9 %collective-permute-start.8 = (bf16[512,1024]{1,0:T(8,128)(2,1)S(1)}, bf16[512,1024]{1,0:T(8,128)(2,1)S(1)}, u32[]{:S(2)}, u32[]{:S(2)}) collective-permute-start(bf16[512,1024]{1,0:T(8,128)(2,1)S(1)} %get-tuple-element.225.refs_0_), channel_id=1, source_target_pairs={{0,1},{1,0},{2,3},{3,2},{4,5},{5,4},{6,7},{7,6},{8,9},{9,8},{10,11... | collective-permute-start | bytes 3145736 | tf_op jit(solution)/shard_map/ppermute | solution.py:29
  5.9 1.6 collective-permute-start.6
  7.5 7.8 %collective-permute-start.7 = (f32[264,128]{1,0:T(8,128)S(1)}, f32[264,128]{1,0:T(8,128)}, u32[]{:S(2)}, u32[]{:S(2)}) collective-permute-start(f32[264,128]{1,0:T(8,128)S(1)} %fusion.19), channel_id=1, source_target_pairs={{0,4},{4,0},{8,12},{12,8},{16,20},{20,16},{24,28},{28,24},{1,5},{5... | collective-permute-start | bytes 405512 | tf_op jit(solution)/shard_map/ppermute | solution.py:29
  10.4 8.6 %copy-start.1 = (bf16[192,1024]{1,0:T(8,128)(2,1)S(1)}, bf16[192,1024]{1,0:T(8,128)(2,1)}, u32[]{:S(2)}) copy-start(bf16[192,1024]{1,0:T(8,128)(2,1)} %copy-done) | copy-start | bytes 1179652
  19.0 2.7 collective-permute-start.11
  19.0 11.5 %collective-permute-start.15 = (bf16[192,1024]{1,0:T(8,128)(2,1)S(1)}, bf16[192,1024]{1,0:T(8,128)(2,1)S(1)}, u32[]{:S(2)}, u32[]{:S(2)}) collective-permute-start(bf16[192,1024]{1,0:T(8,128)(2,1)S(1)} %copy-done.1), channel_id=1, source_target_pairs={{0,2},{1,3},{2,0},{3,1},{4,6},{5,7},{6,4},{7,5},{8,10},{9,11},{10,... | collective-permute-start | bytes 1179656 | tf_op jit(solution)/shard_map/ppermute | solution.py:29
  19.3 6.3 collective-permute-start.9
  30.5 7.2 %collective-permute-start.16 = (bf16[192,1024]{1,0:T(8,128)(2,1)S(1)}, bf16[192,1024]{1,0:T(8,128)(2,1)S(1)}, u32[]{:S(2)}, u32[]{:S(2)}) collective-permute-start(bf16[192,1024]{1,0:T(8,128)(2,1)S(1)} %collective-permute-done.15.refs_0_), channel_id=1, source_target_pairs={{0,1},{1,0},{2,3},{3,2},{4,5},{5,4},{6,7},{7,6},{8,9},{9,8},{10,11... | collective-permute-start | bytes 1179656 | tf_op jit(solution)/shard_map/ppermute | solution.py:29
  30.5 13.4 %collective-permute-start.13 = (bf16[640,256]{1,0:T(8,128)(2,1)S(1)}, bf16[640,256]{1,0:T(8,128)(2,1)S(1)}, u32[]{:S(2)}, u32[]{:S(2)}) collective-permute-start(bf16[640,256]{1,0:T(8,128)(2,1)S(1)} %bitcast.123), channel_id=1, source_target_pairs={{0,4},{4,0},{8,12},{12,8},{16,20},{20,16},{24,28},{28,24},{1,5},{5... | collective-permute-start | bytes 983048 | tf_op jit(solution)/shard_map/ppermute | solution.py:29
  32.0 12.7 %collective-permute-start.14 = (bf16[640,256]{1,0:T(8,128)(2,1)S(1)}, bf16[640,256]{1,0:T(8,128)(2,1)S(1)}, u32[]{:S(2)}, u32[]{:S(2)}) collective-permute-start(bf16[640,256]{1,0:T(8,128)(2,1)S(1)} %bitcast.122), channel_id=1, source_target_pairs={{0,8},{4,12},{8,0},{12,4},{16,24},{20,28},{24,16},{28,20},{1,9},{5... | collective-permute-start | bytes 983048 | tf_op jit(solution)/shard_map/ppermute | solution.py:29
  33.6 10.3 %collective-permute-start.12 = (f32[264,128]{1,0:T(8,128)S(1)}, f32[264,128]{1,0:T(8,128)S(1)}, u32[]{:S(2)}, u32[]{:S(2)}) collective-permute-start(f32[264,128]{1,0:T(8,128)S(1)} %add.136), channel_id=1, source_target_pairs={{0,16},{4,20},{8,24},{12,28},{16,0},{20,4},{24,8},{28,12},{1,17},{... | collective-permute-start | bytes 405512 | tf_op jit(solution)/shard_map/ppermute | solution.py:29
  45.0 11.2 %collective-permute-start.18 = (bf16[704,256]{1,0:T(8,128)(2,1)S(1)}, bf16[704,256]{1,0:T(8,128)(2,1)S(1)}, u32[]{:S(2)}, u32[]{:S(2)}) collective-permute-start(bf16[704,256]{1,0:T(8,128)(2,1)S(1)} %pad_maximum_fusion.2), channel_id=1, source_target_pairs={{0,4},{4,0},{8,12},{12,8},{16,20},{20,16},{24,28},{28,24},{1,5},{5... | collective-permute-start | bytes 1081352 | tf_op jit(solution)/shard_map/ppermute | solution.py:29
  45.6 13.6 %collective-permute-start.19 = (bf16[704,256]{1,0:T(8,128)(2,1)S(1)}, bf16[704,256]{1,0:T(8,128)(2,1)S(1)}, u32[]{:S(2)}, u32[]{:S(2)}) collective-permute-start(bf16[704,256]{1,0:T(8,128)(2,1)S(1)} %pad_maximum_fusion.3), channel_id=1, source_target_pairs={{0,8},{4,12},{8,0},{12,4},{16,24},{20,28},{24,16},{28,20},{1,9},{5... | collective-permute-start | bytes 1081352 | tf_op jit(solution)/shard_map/ppermute | solution.py:29
  51.2 5.1 collective-permute-start.17
  59.2 16.8 %copy-start.3 = (f32[1024,256]{1,0:T(8,128)S(1)}, f32[1024,256]{1,0:T(8,128)}, u32[]{:S(2)}) copy-start(f32[1024,256]{1,0:T(8,128)} %sketch.1) | copy-start | bytes 3145732
  59.4 8.7 %collective-permute-start.20 = (bf16[192,256]{1,0:T(8,128)(2,1)S(1)}, bf16[192,256]{1,0:T(8,128)(2,1)S(1)}, u32[]{:S(2)}, u32[]{:S(2)}) collective-permute-start(bf16[192,256]{1,0:T(8,128)(2,1)S(1)} %bitcast.133), channel_id=1, source_target_pairs={{0,4},{4,0},{8,12},{12,8},{16,20},{20,16},{24,28},{28,24},{1,5},{5... | collective-permute-start | bytes 294920 | tf_op jit(solution)/shard_map/ppermute | solution.py:29
  60.0 9.4 %collective-permute-start.22 = (bf16[320,256]{1,0:T(8,128)(2,1)S(1)}, bf16[320,256]{1,0:T(8,128)(2,1)S(1)}, u32[]{:S(2)}, u32[]{:S(2)}) collective-permute-start(bf16[320,256]{1,0:T(8,128)(2,1)S(1)} %pad_maximum_fusion.5), channel_id=1, source_target_pairs={{0,16},{4,20},{8,24},{12,28},{16,0},{20,4},{24,8},{28,12},{1,17},{... | collective-permute-start | bytes 491528 | tf_op jit(solution)/shard_map/ppermute | solution.py:29
  61.7 6.4 collective-permute-start.21
  69.5 6.5 collective-permute-start.23
  139.3 13.5 %collective-permute-start.1 = (bf16[1024,256]{0,1:T(8,128)(2,1)S(1)}, bf16[1024,256]{0,1:T(8,128)(2,1)S(1)}, u32[]{:S(2)}, u32[]{:S(2)}) collective-permute-start(bf16[1024,256]{0,1:T(8,128)(2,1)S(1)} %pad_maximum_fusion.1), channel_id=1, source_target_pairs={{0,2},{1,3},{2,0},{3,1},{4,6},{5,7},{6,4},{7,5},{8,10},{9,11},{10,... | collective-permute-start | bytes 1572872 | tf_op jit(solution)/shard_map/cond/branch_0_fun/ppermute | solution.py:29
  139.7 13.2 %collective-permute-start = (bf16[1024,256]{0,1:T(8,128)(2,1)S(1)}, bf16[1024,256]{0,1:T(8,128)(2,1)}, u32[]{:S(2)}, u32[]{:S(2)}) collective-permute-start(bf16[1024,256]{0,1:T(8,128)(2,1)S(1)} %pad_maximum_fusion.1), channel_id=1, source_target_pairs={{0,1},{1,0},{2,3},{3,2},{4,5},{5,4},{6,7},{7,6},{8,9},{9,8},{10,11... | collective-permute-start | bytes 1572872 | tf_op jit(solution)/shard_map/cond/branch_0_fun/ppermute | solution.py:29
  152.8 2.0 collective-permute-start.2
  287.3 63.1 %copy-start.2 = (f32[8,256,512]{2,1,0:T(8,128)S(1)}, f32[8,256,512]{2,1,0:T(8,128)}, u32[]{:S(2)}) copy-start(f32[8,256,512]{2,1,0:T(8,128)} %get-tuple-element.173) | copy-start | bytes 12582916 | tf_op jit(solution)/shard_map/cond
  289.3 61.2 %collective-permute-start.3 = (f32[4,256,512]{2,1,0:T(8,128)S(1)}, f32[4,256,512]{2,1,0:T(8,128)S(1)}, u32[]{:S(2)}, u32[]{:S(2)}) collective-permute-start(f32[4,256,512]{2,1,0:T(8,128)S(1)} %slice.125), channel_id=1, source_target_pairs={{0,16},{4,20},{8,24},{12,28},{16,0},{20,4},{24,8},{28,12},{1,17},{... | collective-permute-start | bytes 6291464 | tf_op jit(solution)/shard_map/cond/branch_0_fun/ppermute | solution.py:29
  351.0 310.4 %collective-permute-start.4 = (f32[2,256,512]{2,1,0:T(8,128)S(1)}, f32[2,256,512]{2,1,0:T(8,128)S(1)}, u32[]{:S(2)}, u32[]{:S(2)}) collective-permute-start(f32[2,256,512]{2,1,0:T(8,128)S(1)} %slice.191), channel_id=1, source_target_pairs={{0,8},{4,12},{8,0},{12,4},{16,24},{20,28},{24,16},{28,20},{1,9},{5... | collective-permute-start | bytes 3145736 | tf_op jit(solution)/shard_map/cond/branch_0_fun/ppermute | solution.py:29
  661.7 9.5 %collective-permute-start.5 = (f32[1,256,512]{2,1,0:T(8,128)S(1)}, f32[1,256,512]{2,1,0:T(8,128)S(1)}, u32[]{:S(2)}, u32[]{:S(2)}) collective-permute-start(f32[1,256,512]{2,1,0:T(8,128)S(1)} %slice.193), channel_id=1, source_target_pairs={{0,4},{4,0},{8,12},{12,8},{16,20},{20,16},{24,28},{28,24},{1,5},{5... | collective-permute-start | bytes 1572872 | tf_op jit(solution)/shard_map/cond/branch_0_fun/ppermute | solution.py:29
  671.5 0.8 copy-start.4

commit v2 on v1

--- a/solution.py
+++ b/solution.py
@@ -14,10 +14,9 @@
 SPARE = 4 * 2**20
 GROUP = 4
 NEAR_COST = 200 * 2**20
-EARLY_COST = 1024
-LATE_COST = 1024
+FAR_COST = 200 * 2**20
 FACTOR_COST = 200 * 2**20
-CHUNKS = (160, 96)
+LATE_ROWS = 128
 NEWTON = 2
 
 
@@ -36,7 +35,9 @@
     return found
 
 
-def run_tiles(base, span, per_piece, users, items, owner, meta, tiles, slab, add, buf, sems, order):
+def run_tiles(
+    base, span, per_piece, first_col, users, items, owner, meta, tiles, slab, add, buf, sems, order
+):
     count, row, col = meta[0], meta[1], meta[2]
 
     def relative(t):
@@ -52,7 +53,8 @@
 
     def fetch(i):
         slot = lax.rem(i, SLOTS)
-        return pltpu.make_async_copy(tiles.at[order[i]], buf.at[slot], sems.at[slot])
+        source = tiles.at[order[i], :, pl.ds(first_col, buf.shape[2])]
+        return pltpu.make_async_copy(source, buf.at[slot], sems.at[slot])
 
     for i in range(SLOTS):
         @pl.when(i < live)
@@ -70,7 +72,8 @@
                 buf[lax.rem(first + q, SLOTS)],
                 preferred_element_type=F32,
             )
-            found.append(both)
+            half = both.shape[0] // 2
+            found.append(both[:half] + both[half:])
         for q in range(size):
             add(lax.bitwise_xor(owner[items[order[first + q]]], row), found[q])
         for q in range(size):
@@ -95,18 +98,12 @@
     return finish
 
 
-def split_kernel(sketch, whole, *chunks):
-    flat = sketch[...].T
-    high = flat.astype(BF16)
-    low = (flat - high.astype(F32)).astype(BF16)
-    first = 0
-    for chunk in chunks:
-        kc = chunk.shape[0] // 2
-        for i, part in enumerate((high, low)):
-            rows = part[first : first + kc]
-            chunk[i * kc : (i + 1) * kc, :] = rows
-            whole[2 * first + i * kc : 2 * first + (i + 1) * kc, :] = rows
-        first += kc
+def split_kernel(sketch, flat, whole):
+    width = flat.shape[0]
+    flat[...] = sketch[...].T
+    high = flat[...].astype(BF16)
+    whole[:width, :] = high
+    whole[width:, :] = (flat[...] - high.astype(F32)).astype(BF16)
 
 
 def split_sketch(sketch):
@@ -114,36 +111,65 @@
     vmem = pl.BlockSpec(memory_space=pltpu.VMEM)
     return pl.pallas_call(
         split_kernel,
-        out_shape=[jax.ShapeDtypeStruct((2 * k, users), BF16) for k in (width, *CHUNKS)],
+        out_shape=[
+            jax.ShapeDtypeStruct((width, users), F32),
+            jax.ShapeDtypeStruct((2 * width, users), BF16),
+        ],
         in_specs=[vmem],
-        out_specs=[vmem] * (1 + len(CHUNKS)),
+        out_specs=[vmem] * 2,
         compiler_params=pltpu.CompilerParams(vmem_limit_bytes=16 * 2**20),
     )(sketch)
 
 
+def gram_kernel(flat, packed):
+    n = packed.shape[1]
+    top, low = flat[:n, :], flat[n:, :]
+    second = mmt(low, low)
+    r = lax.broadcasted_iota(jnp.int32, (n, n), 0)
+    c = lax.broadcasted_iota(jnp.int32, (n, n), 1)
+    packed[:n] = jnp.where(r >= c, mmt(top, top), second)
+    packed[n : 2 * n] = mmt(low, top)
+    tail = jnp.sum(jnp.where(r == c, second, 0.0), axis=0, keepdims=True)
+    packed[2 * n :] = jnp.broadcast_to(tail, (8, n))
+
+
+def packed_gram(flat):
+    n = flat.shape[0] // 2
+    vmem = pl.BlockSpec(memory_space=pltpu.VMEM)
+    return pl.pallas_call(
+        gram_kernel,
+        out_shape=jax.ShapeDtypeStruct((2 * n + 8, n), F32),
+        in_specs=[vmem],
+        out_specs=vmem,
+        compiler_params=pltpu.CompilerParams(vmem_limit_bytes=16 * 2**20),
+    )(flat)
+
+
 def fill(slab, pieces, per_piece):
     tile_size = slab.shape[2]
-    for c, piece in enumerate(pieces):
-        for h in range(per_piece):
-            slab[c * per_piece + h] = piece[:, h * tile_size : (h + 1) * tile_size]
+    for c, blocks in enumerate(pieces):
+        first = 0
+        for block in blocks:
+            last = first + block.shape[0]
+            for h in range(per_piece):
+                slab[c * per_piece + h, first:last, :] = block[:, h * tile_size : (h + 1) * tile_size]
+            first = last
 
 
 def near_kernel(span, users, items, owner, meta, *refs):
-    pieces = refs[:span]
+    pieces = [refs[i : i + 1] for i in range(span)]
     tiles = refs[span]
     sums = refs[span + 1 : -4]
     slab, buf, sems, order = refs[-4:]
-    per_piece = pieces[0].shape[1] // tiles.shape[1]
-
-    def add(place, both):
-        first = 0
-        for part in sums:
-            kc = part.shape[1]
-            part[place] += both[first : first + kc] + both[first + kc : first + 2 * kc]
-            first += 2 * kc
+    per_piece = pieces[0][0].shape[1] // tiles.shape[1]
+    width = sums[0].shape[2]
+
+    def add(place, value):
+        for o, part in enumerate(sums):
+            part[place] += value[:, o * width : (o + 1) * width]
 
     finish = run_tiles(
-        0, span, per_piece, users, items, owner, meta, tiles, slab, add, buf, sems, order
+        0, span, per_piece, 0, users, items, owner, meta, tiles, slab, add, buf, sems, order
     )
     for part in sums:
         part[...] = jnp.zeros_like(part)
@@ -151,47 +177,44 @@
     finish()
 
 
-def far_kernel(span, orders, users, items, owner, meta, *refs):
-    pieces = refs[:span]
-    start, tiles = refs[span], refs[span + 1]
-    outs = refs[span + 2 : -5]
-    slab, buf, sems, order, acc = refs[-5:]
-    tile_size = tiles.shape[1]
-    per_piece = pieces[0].shape[1] // tile_size
-    kc = pieces[0].shape[0] // 2
-
-    def add(place, both):
-        acc[place] += both[:kc] + both[kc:]
+def far_kernel(span, bits, first_col, users, items, owner, meta, *refs):
+    blocks = (len(refs) - 9) // span
+    pieces = [refs[i * blocks : (i + 1) * blocks] for i in range(span)]
+    start, tiles, keep, send, slab, buf, sems, order, acc = refs[-9:]
+    per_piece = pieces[0][0].shape[1] // tiles.shape[1]
+
+    def add(place, value):
+        acc[place] += value
 
     finish = run_tiles(
-        span, span, per_piece, users, items, owner, meta, tiles, slab, add, buf, sems, order
+        span, span, per_piece, first_col, users, items, owner, meta, tiles, slab, add, buf, sems, order
     )
     acc[...] = start[...]
     fill(slab, pieces, per_piece)
     finish()
-    width = tile_size // len(orders)
-    for o, bits in enumerate(orders):
-        cut = slice(o * width, (o + 1) * width)
-        for k, place in enumerate(places(bits, 0)):
-            outs[2 * o][k] = acc[place, :, cut]
-        for k, place in enumerate(places(bits, 1)):
-            outs[2 * o + 1][k] = acc[place, :, cut].astype(BF16)
+    for k, place in enumerate(places(bits, 0)):
+        keep[k] = acc[place]
+    for k, place in enumerate(places(bits, 1)):
+        send[k] = acc[place].astype(BF16)
 
 
 def tile_call(kernel, scalars, pieces, extra, tiles, shapes, scratch, cost):
     users = scalars[0].shape[0]
     tile_size = tiles.shape[1]
-    blocks = len(pieces) * pieces[0].shape[1] // tile_size
+    flat = [block for blocks in pieces for block in blocks]
+    count = len(pieces) * flat[0].shape[1] // tile_size
+    rows = sum(block.shape[0] for block in pieces[0])
+    cols = tile_size if len(shapes) == 2 and not extra else extra[0].shape[2]
     smem = pl.BlockSpec(memory_space=pltpu.SMEM)
     vmem = pl.BlockSpec(memory_space=pltpu.VMEM)
-    slab = jax.ShapeDtypeStruct((blocks, pieces[0].shape[0], tile_size), BF16)
-    buf = jax.ShapeDtypeStruct((SLOTS, tile_size, tile_size), BF16)
-    held = sum(x.size * x.dtype.itemsize for x in (*pieces, *extra, *shapes, *scratch, slab, buf))
+    slab = jax.ShapeDtypeStruct((count, rows, tile_size), BF16)
+    buf = jax.ShapeDtypeStruct((SLOTS, tile_size, cols), BF16)
+    held = sum(x.size * x.dtype.itemsize for x in (*flat, *extra, *shapes, *scratch, slab, buf))
     return pl.pallas_call(
         kernel,
         out_shape=shapes,
         in_specs=[smem] * len(scalars)
-        + [vmem] * (len(pieces) + len(extra))
+        + [vmem] * (len(flat) + len(extra))
         + [pl.BlockSpec(memory_space=pl.ANY)],
         out_specs=[vmem] * len(shapes),
         scratch_shapes=[
@@ -203,33 +226,40 @@
         + [pltpu.VMEM(x.shape, x.dtype) for x in scratch],
         compiler_params=pltpu.CompilerParams(vmem_limit_bytes=held + SPARE),
         cost_estimate=pl.CostEstimate(flops=0, bytes_accessed=cost, transcendentals=0),
-    )(*scalars, *pieces, *extra, tiles)
-
-
-def near_sums(scalars, pieces, tiles, rows):
+    )(*scalars, *flat, *extra, tiles)
+
+
+def near_sums(scalars, pieces, tiles, rows, parts):
     tile_size = tiles.shape[1]
-    shapes = [jax.ShapeDtypeStruct((rows, kc, tile_size), F32) for kc in CHUNKS]
+    width = pieces[0].shape[0] // 2
+    shapes = [jax.ShapeDtypeStruct((rows, width, tile_size // parts), F32)] * parts
     return tile_call(
-        functools.partial(near_kernel, len(pieces)), scalars, pieces, [], tiles, shapes, [], NEAR_COST
-    )
-
-
-def far_sums(scalars, pieces, start, tiles, orders, cost):
-    rows, kc, tile_size = start.shape
-    width = tile_size // len(orders)
-    shapes = []
-    for _ in orders:
-        shapes.append(jax.ShapeDtypeStruct((rows // 2, kc, width), F32))
-        shapes.append(jax.ShapeDtypeStruct((rows // 2, kc, width), BF16))
+        functools.partial(near_kernel, len(pieces)),
+        scalars,
+        [[piece] for piece in pieces],
+        [],
+        tiles,
+        shapes,
+        [],
+        NEAR_COST,
+    )
+
+
+def far_sums(scalars, pieces, start, tiles, bits, first_col):
+    rows, width, cols = start.shape
+    shapes = [
+        jax.ShapeDtypeStruct((rows // 2, width, cols), F32),
+        jax.ShapeDtypeStruct((rows // 2, width, cols), BF16),
+    ]
     return tile_call(
-        functools.partial(far_kernel, len(pieces), orders),
+        functools.partial(far_kernel, len(pieces), bits, first_col),
         scalars,
         pieces,
         [start],
         tiles,
         shapes,
         [jax.ShapeDtypeStruct(start.shape, F32)],
-        cost,
+        FAR_COST,
     )
 
 
@@ -291,10 +321,10 @@
     )(packed)
 
 
-def last_kernel(inverse, early, keep0, keep1, came, out):
+def last_kernel(inverse, keep0, keep1, came, out):
     left = keep0[0] + came[0].astype(F32)
     right = keep1[0] + came[1].astype(F32)
-    total = jnp.concatenate([early[...], jnp.concatenate([left, right], axis=1)], axis=0)
+    total = jnp.concatenate([left, right], axis=1)
     w = inverse[...]
     wh, th = w.astype(BF16), total.astype(BF16)
     wl = (w - wh.astype(F32)).astype(BF16)
@@ -303,24 +333,15 @@
     out[...] = jnp.dot(wh, th, preferred_element_type=F32) + small
 
 
-def last(inverse, early, keeps, came):
+def last(inverse, keeps, came):
     vmem = pl.BlockSpec(memory_space=pltpu.VMEM)
     return pl.pallas_call(
         last_kernel,
-        out_shape=jax.ShapeDtypeStruct((inverse.shape[0], early.shape[1]), F32),
-        in_specs=[vmem] * 5,
+        out_shape=jax.ShapeDtypeStruct((inverse.shape[0], 2 * came.shape[2]), F32),
+        in_specs=[vmem] * 4,
         out_specs=vmem,
         compiler_params=pltpu.CompilerParams(vmem_limit_bytes=16 * 2**20),
-    )(inverse, early, *keeps, came)
-
-
-def pack(gram):
-    n = gram.shape[0] // 2
-    r = lax.broadcasted_iota(jnp.int32, (n, n), 0)
-    c = lax.broadcasted_iota(jnp.int32, (n, n), 1)
-    mixed = jnp.where(r >= c, gram[:n, :n], gram[n:, n:])
-    tail = jnp.sum(jnp.where(r == c, gram[n:, n:], 0.0), axis=0, keepdims=True)
-    return jnp.concatenate([mixed, gram[n:, :n], jnp.broadcast_to(tail, (8, n))], axis=0)
+    )(inverse, *keeps, came)
 
 
 def full_path(rows, cols, sketch, tiles, tile_user, tile_item, tile_count, item_owner, packed):
@@ -409,66 +430,50 @@
 
     fence = lax.optimization_barrier
     far = far_bit
-    whole, *chunks = split_sketch(sketch)
+    flat, whole = split_sketch(sketch)
     near = spread(whole)
-    crossed = [swap(chunk, "cols", cols, far) for chunk in chunks]
-    gram = lax.dot_general(
-        sketch, sketch, (((0,), (0,)), ((), ())), precision=HIGH, preferred_element_type=F32
-    )
-    packed = pack(gram)
+    crossed = [
+        swap(part, "cols", cols, far) for part in (whole[:-LATE_ROWS], whole[-LATE_ROWS:])
+    ]
+    packed = packed_gram(flat)
     for bit in near_bits:
         packed = packed + swap(packed, "cols", cols, bit)
     came = swap(packed, "rows", rows, 1)
     near[0] = after(near[0], packed)
-    sums = near_sums(scalars, near, tiles, rows)
+    sums = near_sums(scalars, near, tiles, rows, len(orders))
     packed, came, *sums = fence((packed, came, *sums))
     packed = packed + came
-    came = swap(packed, "rows", rows, 2)
-    crossed[0] = after(crossed[0], packed)
-    outs = far_sums(scalars, spread(crossed[0]), sums[0], tiles, orders, EARLY_COST)
-    packed, came, *outs = fence((packed, came, *outs))
-    packed = packed + came
-    came = swap(packed, "rows", rows, 4)
-    lanes = [(outs[2 * o], outs[2 * o + 1], order[0]) for o, order in enumerate(orders)]
+    for b in range(1, row_bits):
+        packed = packed + swap(packed, "rows", rows, 1 << b)
+        if b == row_bits - 1:
+            _, *crossed = fence((packed, *crossed))
+    parts = [spread(c) for c in crossed]
+    parts[0][0] = after(parts[0][0], packed)
+    pieces = list(zip(*parts))
+    cut = tiles.shape[2] // len(orders)
+    last_pair = far_sums(scalars, pieces, sums[1], tiles, orders[1], cut)
+    came = swap(packed, "cols", cols, far)
+    lanes = [(*last_pair, orders[1][0])]
     groups = exchange(lanes, rows)
-    crossed[1] = after(crossed[1], packed)
-    later = far_sums(scalars, spread(crossed[1]), sums[1], tiles, orders, LATE_COST)
-    flying = [g[1] for g in groups]
-    packed, came, *rest = fence((packed, came, *flying, *later))
-    groups = [(g[0], x) for g, x in zip(groups, rest)]
-    later = rest[len(groups) :]
-    packed = packed + came
-    stages = [("cols", far)] + [("rows", 1 << b) for b in range(3, row_bits)]
-
+    first_pair = far_sums(scalars, pieces, after(sums[0], last_pair[1]), tiles, orders[0], 0)
+    packed = packed + after(came, first_pair[1])
+    lanes.append((*first_pair, orders[0][0]))
+    groups.append(([1], exchange(lanes[1:], rows)[0][1]))
+    inverse, good = factor(after(packed, first_pair[1]))
+    flying = fence((inverse, *[g[1] for g in groups]))
+    inverse = flying[0]
+    groups = [(g[0], x) for g, x in zip(groups, flying[1:])]
     totals = received(lanes, groups)
-    late = [(later[2 * o], later[2 * o + 1]) for o in range(len(orders))]
-    for step in range(1, row_bits + 1):
-        lanes = []
-        if step < row_bits:
-            lanes += [(*split(t), order[step]) for t, order in zip(totals, orders)]
-        lanes += [(*pair, order[step - 1]) for pair, order in zip(late, orders)]
+    for step in range(1, row_bits):
+        lanes = [(*split(t), order[step]) for t, order in zip(totals, orders[::-1])]
         groups = exchange(lanes, rows)
-        flying = [g[1] for g in groups]
-        if step <= len(stages):
-            axis, bit = stages[step - 1]
-            came = swap(packed, axis, rows if axis == "rows" else cols, bit)
-            packed, came, *flying = fence((packed, came, *flying))
-            packed = packed + came
-        if step == len(stages) + 1:
-            inverse, good = factor(after(packed, *[lane[1] for lane in lanes]))
-            inverse, *flying = fence((inverse, *flying))
-        groups = [(g[0], x) for g, x in zip(groups, flying)]
-        if step < row_bits:
-            new = received(lanes, groups)
-            totals, new = new[: len(orders)], new[len(orders) :]
-            late = [split(t) for t in new]
-        if step == row_bits - 1:
-            early = jnp.concatenate([t[0] for t in totals], axis=1)
-    keeps = [lane[0] for lane in lanes]
-    came = groups[0][1].reshape(len(lanes), *lanes[0][1].shape[1:])
+        if step < row_bits - 1:
+            totals = received(lanes, groups)
+    keeps = [lane[0] for lane in lanes[::-1]]
+    came = groups[0][1].reshape(len(lanes), *lanes[0][1].shape[1:])[::-1]
     out = lax.cond(
         good[0] > 0,
-        lambda: last(inverse, early, keeps, came),
+        lambda: last(inverse, keeps, came),
         lambda: full_path(rows, cols, sketch, tiles, tile_user, tile_item, tile_count, item_owner, packed),
     )
     return out[None, None]

time: 682 us -> 694 us (1.018)
  the two profiles are of different devices: /device:TPU:2 before, /device:TPU:16 now
where the time goes in v2:
time: 694 us; the launch traced here: 690 us
  starting transfers between devices  364 us (52%)
  waiting for transfers between devices  181 us (26%)
  other arithmetic  58.4 us (8%)
  loops' own time  32.3 us (5%)
  local copies, waits for them, and re-layouts  26 us (4%)
  Pallas kernels  13.5 us (2%)
  matrix products  13.5 us (2%)
    ppermute x21, starting transfers between devices, swap(): return lax.ppermute(x, axis, [(i, i ^ bit) for i in range(count)])  364 us
    ppermute x21, waiting for transfers between devices, swap(): return lax.ppermute(x, axis, [(i, i ^ bit) for i in range(count)])  181 us
    another operation x6, other arithmetic, full_path(): lower = jnp.linalg.cholesky(gram)  34.1 us
    another operation x1, loops' own time, full_path(): totals = lax.fori_loop(0, tile_count[0], step, totals)  30.1 us
    another operation x5, other arithmetic, full_path(): lax.linalg.triangular_solve(lower, sketch, left_side=False, lower=True, t...  19.8 us
  transfers between devices with their start and end apart: 21, of which 17 were waited for; matrix products, arithmetic and copies ran while one was open for 0% of the time, Pallas kernels for 1%

profile of v2, /device:TPU:16, one launch (start us, length us, event | category | flops | bytes accessed | tf_op | source)
XLA Modules:
  0.0 689.9 jit_solution(15539007641426399917)
XLA Ops:
  0.0 1.6 shard_map.66
  2.7 1.5 collective-permute-start.12
  4.2 1.4 shard_map.67
  5.9 1.1 collective-permute-done.6
  7.0 1.6 collective-permute-start.7
  9.4 2.5 shard_map.68
  12.8 1.6 collective-permute-start.9
  15.1 3.9 collective-permute-done.9
  19.7 6.8 collective-permute-done.10
  26.5 2.0 collective-permute-done.13.refs_1_
  29.0 2.1 collective-permute-done.15.refs_3_
  31.1 2.1 shard_map.69
  33.2 2.1 shard_map.70
  35.3 3.1 collective-permute-start.17
  38.5 1.7 collective-permute-start.11
  40.2 3.3 collective-permute-done.11
  43.5 3.8 shard_map.71
  47.4 2.5 collective-permute-done.17
  49.9 2.4 collective-permute-done.16
  53.0 1.8 collective-permute-start.19
  54.8 5.4 collective-permute-done.18
  61.3 8.8 %collective-permute-start.20 = (bf16[512,256]{1,0:T(8,128)(2,1)S(1)}, bf16[512,256]{1,0:T(8,128)(2,1)S(1)}, u32[]{:S(2)}, u32[]{:S(2)}) collective-permute-start(bf16[512,256]{1,0:T(8,128)(2,1)S(1)} %pad_maximum_fusion.2), channel_id=1, source_target_pairs={{0,16},{4,20},{8,24},{12,28},{16,0},{20,4},{24,8},{28,12},{1,17},{... | collective-permute-start | bytes 786440 | tf_op jit(solution)/shard_map/ppermute | solution.py:28
  70.7 9.8 %collective-permute-done.20 = bf16[512,256]{1,0:T(8,128)(2,1)S(1)} collective-permute-done((bf16[512,256]{1,0:T(8,128)(2,1)S(1)}, bf16[512,256]{1,0:T(8,128)(2,1)S(1)}, u32[]{:S(2)}, u32[]{:S(2)}) %collective-permute-start.20) | collective-permute-done | bytes 262176 | tf_op jit(solution)/shard_map/ppermute | solution.py:28
  80.5 608.5 %conditional.1 = (f32[1,1,256,512]{3,2,1,0:T(8,128)S(1)}) conditional(s32[]{:T(128)} %bitcast.22, (s32[1]{0:T(128)}, f32[264,128]{1,0:T(8,128)S(1)}, f32[1024,256]{1,0:T(8,128)S(1)}, s32[1,8]{1,0:T(1,128)S(1)}, s32[40]{0:T(128)S(1)}, /*index=5*/s32[40]{0:T(128)S(1)}, bf16[40,512,512]{2,1,0:T(8,128)(2,1)}) %tuple.87, (f32[2,256,256]{2,1,0:T(8,128)S(1)}, ...), branch_computations={%region_0.7_spmd, %region_7.8_spmd} | conditional | flops 802537728 | bytes 80229168 | solution.py:474
  81.4 11.7 %cholesky.8 = f32[128,128]{1,0:T(8,128)S(1)} custom-call(f32[128,128]{1,0:T(8,128)S(1)} %cholesky.47), custom_call_target="Cholesky" | custom-call | tf_op jit(solution)/shard_map/cond/branch_0_fun/jit(cholesky)/cholesky | solution.py:355
  93.5 9.8 %custom-call.12 = f32[1,128,128]{1,2,0:T(8,128)S(1)} custom-call(f32[1,128,128]{2,1,0:T(8,128)S(1)} %copy.15), custom_call_target="InvertDiagBlocksLowerTriangular" | custom-call | tf_op jit(solution)/shard_map/cond/branch_0_fun/jit(cholesky)/cholesky | solution.py:355
  103.8 11.7 %cholesky.30 = f32[128,128]{1,0:T(8,128)S(1)} custom-call(f32[128,128]{1,0:T(8,128)S(1)} %convolution_subtract_fusion.1), custom_call_target="Cholesky" | custom-call | tf_op jit(solution)/shard_map/cond/branch_0_fun/jit(cholesky)/cholesky | solution.py:355
  117.7 4.0 while.13
  118.5 1.3 bitcast_dynamic-update-slice_fusion.2
  120.4 1.3 bitcast_dynamic-update-slice_fusion.2
  121.6 19.7 %custom-call.13 = f32[2,128,128]{1,2,0:T(8,128)S(1)} custom-call(f32[2,128,128]{2,1,0:T(8,128)S(1)} %get-tuple-element.231), custom_call_target="InvertDiagBlocksLowerTriangular" | custom-call | tf_op jit(solution)/shard_map/cond/branch_0_fun/triangular_solve | solution.py:356
  143.8 12.7 %collective-permute-done.1 = bf16[1024,256]{0,1:T(8,128)(2,1)S(1)} collective-permute-done((bf16[1024,256]{0,1:T(8,128)(2,1)S(1)}, bf16[1024,256]{0,1:T(8,128)(2,1)S(1)}, u32[]{:S(2)}, u32[]{:S(2)}) %collective-permute-start.1) | collective-permute-done | bytes 524320 | tf_op jit(solution)/shard_map/cond/branch_0_fun/ppermute | solution.py:28
  157.3 1.2 collective-permute-done.2
  158.5 3.1 pad_maximum_fusion
  161.6 2.5 broadcast.96
  164.1 55.1 %while.12 = (s32[]{:T(128)}, f32[8,256,512]{2,1,0:T(8,128)}, s32[]{:T(128)}, s32[40]{0:T(128)S(1)}, s32[8]{0:T(128)S(1)}, /*index=5*/s32[]{:T(128)}, s32[40]{0:T...) while((s32[]{:T(128)}, f32[8,256,512]{2,1,0:T(8,128)}, ...), condition=%wide.region_6.6_spmd, body=%wide.region_5.5_spmd.sunk | while | flops 134348832 | bytes 2884192 | solution.py:378
  172.8 2.2 fusion.28
  183.7 2.1 fusion.28
  194.6 2.1 fusion.28
  205.5 2.1 fusion.28
  216.4 2.1 fusion.28
  219.2 1.9 slice.90
  221.1 25.2 %collective-permute-start.3 = (f32[4,256,512]{2,1,0:T(8,128)S(1)}, f32[4,256,512]{2,1,0:T(8,128)S(1)}, u32[]{:S(2)}, u32[]{:S(2)}) collective-permute-start(f32[4,256,512]{2,1,0:T(8,128)S(1)} %slice.90), channel_id=1, source_target_pairs={{0,16},{4,20},{8,24},{12,28},{16,0},{20,4},{24,8},{28,12},{1,17},{... | collective-permute-start | bytes 6291464 | tf_op jit(solution)/shard_map/cond/branch_0_fun/ppermute | solution.py:28
  246.4 90.2 %collective-permute-done.3 = f32[4,256,512]{2,1,0:T(8,128)S(1)} collective-permute-done((f32[4,256,512]{2,1,0:T(8,128)S(1)}, f32[4,256,512]{2,1,0:T(8,128)S(1)}, u32[]{:S(2)}, u32[]{:S(2)}) %collective-permute-start.3) | collective-permute-done | bytes 2097184 | tf_op jit(solution)/shard_map/cond/branch_0_fun/ppermute | solution.py:28
  337.2 2.6 collective-permute-start.4
  339.8 23.4 %collective-permute-done.4 = f32[2,256,512]{2,1,0:T(8,128)S(1)} collective-permute-done((f32[2,256,512]{2,1,0:T(8,128)S(1)}, f32[2,256,512]{2,1,0:T(8,128)S(1)}, u32[]{:S(2)}, u32[]{:S(2)}) %collective-permute-start.4) | collective-permute-done | bytes 1048608 | tf_op jit(solution)/shard_map/cond/branch_0_fun/ppermute | solution.py:28
  363.5 313.1 %collective-permute-start.5 = (f32[1,256,512]{2,1,0:T(8,128)S(1)}, f32[1,256,512]{2,1,0:T(8,128)S(1)}, u32[]{:S(2)}, u32[]{:S(2)}) collective-permute-start(f32[1,256,512]{2,1,0:T(8,128)S(1)} %slice.128), channel_id=1, source_target_pairs={{0,4},{4,0},{8,12},{12,8},{16,20},{20,16},{24,28},{28,24},{1,5},{5... | collective-permute-start | bytes 1572872 | tf_op jit(solution)/shard_map/cond/branch_0_fun/ppermute | solution.py:28
  676.6 12.1 %collective-permute-done.5 = f32[1,256,512]{2,1,0:T(8,128)S(1)} collective-permute-done((f32[1,256,512]{2,1,0:T(8,128)S(1)}, f32[1,256,512]{2,1,0:T(8,128)S(1)}, u32[]{:S(2)}, u32[]{:S(2)}) %collective-permute-start.5) | collective-permute-done | bytes 524320 | tf_op jit(solution)/shard_map/cond/branch_0_fun/ppermute | solution.py:28
  (109 shorter events, 28.9 us)
Async XLA Ops:
  0.0 9.4 %copy-start.6 = (s32[40]{0:T(128)S(1)}, s32[40]{0:T(128)}, u32[]{:S(2)}) copy-start(s32[40]{0:T(128)} %items.5) | copy-start | bytes 484
  0.0 9.4 %copy-start.7 = (s32[40]{0:T(128)S(1)}, s32[40]{0:T(128)}, u32[]{:S(2)}) copy-start(s32[40]{0:T(128)} %users.5) | copy-start | bytes 484
  0.0 9.4 %copy-start.5 = (s32[1,8]{1,0:T(1,128)S(1)}, s32[1,8]{1,0:T(1,128)}, u32[]{:S(2)}) copy-start(s32[1,8]{1,0:T(1,128)} %param.15) | copy-start | bytes 100
  1.6 7.7 %collective-permute-start.8 = (bf16[512,1024]{1,0:T(8,128)(2,1)S(1)}, bf16[512,1024]{1,0:T(8,128)(2,1)S(1)}, u32[]{:S(2)}, u32[]{:S(2)}) collective-permute-start(bf16[512,1024]{1,0:T(8,128)(2,1)S(1)} %get-tuple-element.201.refs_0_), channel_id=1, source_target_pairs={{0,1},{1,0},{2,3},{3,2},{4,5},{5,4},{6,7},{7,6},{8,9},{9,8},{10,11... | collective-permute-start | bytes 3145736 | tf_op jit(solution)/shard_map/ppermute | solution.py:28
  2.7 25.8 %collective-permute-start.12 = (bf16[384,1024]{1,0:T(8,128)(2,1)}, bf16[384,1024]{1,0:T(8,128)(2,1)S(1)}, u32[]{:S(2)}, u32[]{:S(2)}) collective-permute-start(bf16[384,1024]{1,0:T(8,128)(2,1)} %slice.105), channel_id=1, source_target_pairs={{0,2},{1,3},{2,0},{3,1},{4,6},{5,7},{6,4},{7,5},{8,10},{9,11},{10,... | collective-permute-start | bytes 2359304 | tf_op jit(solution)/shard_map/ppermute | solution.py:28
  5.6 1.4 collective-permute-start.6
  7.0 5.8 collective-permute-start.7
  9.4 21.8 %copy-start = (bf16[40,512,512]{2,1,0:T(8,128)(2,1)S(1)}, bf16[40,512,512]{2,1,0:T(8,128)(2,1)}, u32[]{:S(2)}) copy-start(bf16[40,512,512]{2,1,0:T(8,128)(2,1)} %refs_5_.3) | copy-start | bytes 62914564
  12.8 6.2 collective-permute-start.9
  14.5 14.0 %collective-permute-start.13 = (bf16[128,1024]{1,0:T(8,128)(2,1)S(1)}, bf16[128,1024]{1,0:T(8,128)(2,1)S(1)}, u32[]{:S(2)}, u32[]{:S(2)}) collective-permute-start(bf16[128,1024]{1,0:T(8,128)(2,1)S(1)} %slice.106), channel_id=1, source_target_pairs={{0,2},{1,3},{2,0},{3,1},{4,6},{5,7},{6,4},{7,5},{8,10},{9,11},{10,... | collective-permute-start | bytes 786440 | tf_op jit(solution)/shard_map/ppermute | solution.py:28
  19.0 7.4 %collective-permute-start.10 = (f32[264,128]{1,0:T(8,128)S(1)}, f32[264,128]{1,0:T(8,128)S(1)}, u32[]{:S(2)}, u32[]{:S(2)}) collective-permute-start(f32[264,128]{1,0:T(8,128)S(1)} %add.118), channel_id=1, source_target_pairs={{0,16},{4,20},{8,24},{12,28},{16,0},{20,4},{24,8},{28,12},{1,17},{... | collective-permute-start | bytes 405512 | tf_op jit(solution)/shard_map/ppermute | solution.py:28
  28.5 2.7 collective-permute-start.14
  28.5 2.7 collective-permute-start.15
  35.3 14.6 %collective-permute-start.17 = (bf16[1024,256]{1,0:T(8,128)(2,1)S(1)}, bf16[1024,256]{1,0:T(8,128)(2,1)S(1)}, u32[]{:S(2)}, u32[]{:S(2)}) collective-permute-start(bf16[1024,256]{1,0:T(8,128)(2,1)S(1)} %bitcast.93), channel_id=1, source_target_pairs={{0,4},{4,0},{8,12},{12,8},{16,20},{20,16},{24,28},{28,24},{1,5},{5... | collective-permute-start | bytes 1572872 | tf_op jit(solution)/shard_map/ppermute | solution.py:28
  38.3 13.9 %collective-permute-start.16 = (bf16[1024,256]{1,0:T(8,128)(2,1)S(1)}, bf16[1024,256]{1,0:T(8,128)(2,1)S(1)}, u32[]{:S(2)}, u32[]{:S(2)}) collective-permute-start(bf16[1024,256]{1,0:T(8,128)(2,1)S(1)} %bitcast.92), channel_id=1, source_target_pairs={{0,8},{4,12},{8,0},{12,4},{16,24},{20,28},{24,16},{28,20},{1,9},{5... | collective-permute-start | bytes 1572872 | tf_op jit(solution)/shard_map/ppermute | solution.py:28
  38.5 5.0 collective-permute-start.11
  52.4 28.1 %copy-start.2 = (f32[1024,256]{1,0:T(8,128)S(1)}, f32[1024,256]{1,0:T(8,128)}, u32[]{:S(2)}) copy-start(f32[1024,256]{1,0:T(8,128)} %sketch.1) | copy-start | bytes 3145732
  52.4 7.8 %collective-permute-start.18 = (bf16[512,256]{1,0:T(8,128)(2,1)S(1)}, bf16[512,256]{1,0:T(8,128)(2,1)S(1)}, u32[]{:S(2)}, u32[]{:S(2)}) collective-permute-start(bf16[512,256]{1,0:T(8,128)(2,1)S(1)} %bitcast.99), channel_id=1, source_target_pairs={{0,8},{4,12},{8,0},{12,4},{16,24},{20,28},{24,16},{28,20},{1,9},{5... | collective-permute-start | bytes 786440 | tf_op jit(solution)/shard_map/ppermute | solution.py:28
  53.0 8.1 %collective-permute-start.19 = (bf16[512,256]{1,0:T(8,128)(2,1)S(1)}, bf16[512,256]{1,0:T(8,128)(2,1)S(1)}, u32[]{:S(2)}, u32[]{:S(2)}) collective-permute-start(bf16[512,256]{1,0:T(8,128)(2,1)S(1)} %bitcast.101), channel_id=1, source_target_pairs={{0,4},{4,0},{8,12},{12,8},{16,20},{20,16},{24,28},{28,24},{1,5},{5... | collective-permute-start | bytes 786440 | tf_op jit(solution)/shard_map/ppermute | solution.py:28
  61.3 19.2 %collective-permute-start.20 = (bf16[512,256]{1,0:T(8,128)(2,1)S(1)}, bf16[512,256]{1,0:T(8,128)(2,1)S(1)}, u32[]{:S(2)}, u32[]{:S(2)}) collective-permute-start(bf16[512,256]{1,0:T(8,128)(2,1)S(1)} %pad_maximum_fusion.2), channel_id=1, source_target_pairs={{0,16},{4,20},{8,24},{12,28},{16,0},{20,4},{24,8},{28,12},{1,17},{... | collective-permute-start | bytes 786440 | tf_op jit(solution)/shard_map/ppermute | solution.py:28
  143.7 12.8 %collective-permute-start.1 = (bf16[1024,256]{0,1:T(8,128)(2,1)S(1)}, bf16[1024,256]{0,1:T(8,128)(2,1)S(1)}, u32[]{:S(2)}, u32[]{:S(2)}) collective-permute-start(bf16[1024,256]{0,1:T(8,128)(2,1)S(1)} %pad_maximum_fusion.1), channel_id=1, source_target_pairs={{0,2},{1,3},{2,0},{3,1},{4,6},{5,7},{6,4},{7,5},{8,10},{9,11},{10,... | collective-permute-start | bytes 1572872 | tf_op jit(solution)/shard_map/cond/branch_0_fun/ppermute | solution.py:28
  143.8 12.7 %collective-permute-start = (bf16[1024,256]{0,1:T(8,128)(2,1)S(1)}, bf16[1024,256]{0,1:T(8,128)(2,1)S(1)}, u32[]{:S(2)}, u32[]{:S(2)}) collective-permute-start(bf16[1024,256]{0,1:T(8,128)(2,1)S(1)} %pad_maximum_fusion.1), channel_id=1, source_target_pairs={{0,1},{1,0},{2,3},{3,2},{4,5},{5,4},{6,7},{7,6},{8,9},{9,8},{10,11... | collective-permute-start | bytes 1572872 | tf_op jit(solution)/shard_map/cond/branch_0_fun/ppermute | solution.py:28
  156.5 2.0 collective-permute-start.2
  156.5 0.8 copy-start.4
  219.2 117.4 %copy-start.1 = (f32[8,256,512]{2,1,0:T(8,128)S(1)}, f32[8,256,512]{2,1,0:T(8,128)}, u32[]{:S(2)}) copy-start(f32[8,256,512]{2,1,0:T(8,128)} %get-tuple-element.170) | copy-start | bytes 12582916 | tf_op jit(solution)/shard_map/cond
  221.1 115.5 %collective-permute-start.3 = (f32[4,256,512]{2,1,0:T(8,128)S(1)}, f32[4,256,512]{2,1,0:T(8,128)S(1)}, u32[]{:S(2)}, u32[]{:S(2)}) collective-permute-start(f32[4,256,512]{2,1,0:T(8,128)S(1)} %slice.90), channel_id=1, source_target_pairs={{0,16},{4,20},{8,24},{12,28},{16,0},{20,4},{24,8},{28,12},{1,17},{... | collective-permute-start | bytes 6291464 | tf_op jit(solution)/shard_map/cond/branch_0_fun/ppermute | solution.py:28
  337.2 26.1 %collective-permute-start.4 = (f32[2,256,512]{2,1,0:T(8,128)S(1)}, f32[2,256,512]{2,1,0:T(8,128)S(1)}, u32[]{:S(2)}, u32[]{:S(2)}) collective-permute-start(f32[2,256,512]{2,1,0:T(8,128)S(1)} %slice.126), channel_id=1, source_target_pairs={{0,8},{4,12},{8,0},{12,4},{16,24},{20,28},{24,16},{28,20},{1,9},{5... | collective-permute-start | bytes 3145736 | tf_op jit(solution)/shard_map/cond/branch_0_fun/ppermute | solution.py:28
  363.5 325.2 %collective-permute-start.5 = (f32[1,256,512]{2,1,0:T(8,128)S(1)}, f32[1,256,512]{2,1,0:T(8,128)S(1)}, u32[]{:S(2)}, u32[]{:S(2)}) collective-permute-start(f32[1,256,512]{2,1,0:T(8,128)S(1)} %slice.128), channel_id=1, source_target_pairs={{0,4},{4,0},{8,12},{12,8},{16,20},{20,16},{24,28},{28,24},{1,5},{5... | collective-permute-start | bytes 1572872 | tf_op jit(solution)/shard_map/cond/branch_0_fun/ppermute | solution.py:28
  689.1 0.8 copy-start.3

commit v3 on v1

--- a/solution.py
+++ b/solution.py
@@ -95,17 +95,18 @@
     return finish
 
 
-def split_kernel(sketch, whole, *chunks):
-    flat = sketch[...].T
-    high = flat.astype(BF16)
-    low = (flat - high.astype(F32)).astype(BF16)
+def split_kernel(sketch, flat, whole, chunk):
+    flat[...] = sketch[...].T
     first = 0
-    for chunk in chunks:
-        kc = chunk.shape[0] // 2
+    for kc in CHUNKS:
+        rows = flat[first : first + kc, :]
+        high = rows.astype(BF16)
+        low = (rows - high.astype(F32)).astype(BF16)
         for i, part in enumerate((high, low)):
-            rows = part[first : first + kc]
-            chunk[i * kc : (i + 1) * kc, :] = rows
-            whole[2 * first + i * kc : 2 * first + (i + 1) * kc, :] = rows
+            start = 2 * first + i * kc
+            whole[start : start + kc, :] = part
+            if first == 0:
+                chunk[start : start + kc, :] = part
         first += kc
 
 
@@ -114,11 +115,36 @@
     vmem = pl.BlockSpec(memory_space=pltpu.VMEM)
     return pl.pallas_call(
         split_kernel,
-        out_shape=[jax.ShapeDtypeStruct((2 * k, users), BF16) for k in (width, *CHUNKS)],
+        out_shape=[jax.ShapeDtypeStruct((width, users), F32)]
+        + [jax.ShapeDtypeStruct((2 * k, users), BF16) for k in (width, CHUNKS[0])],
         in_specs=[vmem],
-        out_specs=[vmem] * (1 + len(CHUNKS)),
+        out_specs=[vmem] * 3,
         compiler_params=pltpu.CompilerParams(vmem_limit_bytes=16 * 2**20),
     )(sketch)
+
+
+def gram_kernel(flat, packed):
+    n = packed.shape[1]
+    top, low = flat[:n, :], flat[n:, :]
+    second = mmt(low, low)
+    r = lax.broadcasted_iota(jnp.int32, (n, n), 0)
+    c = lax.broadcasted_iota(jnp.int32, (n, n), 1)
+    packed[:n] = jnp.where(r >= c, mmt(top, top), second)
+    packed[n : 2 * n] = mmt(low, top)
+    tail = jnp.sum(jnp.where(r == c, second, 0.0), axis=0, keepdims=True)
+    packed[2 * n :] = jnp.broadcast_to(tail, (8, n))
+
+
+def packed_gram(flat):
+    n = flat.shape[0] // 2
+    vmem = pl.BlockSpec(memory_space=pltpu.VMEM)
+    return pl.pallas_call(
+        gram_kernel,
+        out_shape=jax.ShapeDtypeStruct((2 * n + 8, n), F32),
+        in_specs=[vmem],
+        out_specs=vmem,
+        compiler_params=pltpu.CompilerParams(vmem_limit_bytes=16 * 2**20),
+    )(flat)
 
 
 def fill(slab, pieces, per_piece):
@@ -314,15 +340,6 @@
     )(inverse, early, *keeps, came)
 
 
-def pack(gram):
-    n = gram.shape[0] // 2
-    r = lax.broadcasted_iota(jnp.int32, (n, n), 0)
-    c = lax.broadcasted_iota(jnp.int32, (n, n), 1)
-    mixed = jnp.where(r >= c, gram[:n, :n], gram[n:, n:])
-    tail = jnp.sum(jnp.where(r == c, gram[n:, n:], 0.0), axis=0, keepdims=True)
-    return jnp.concatenate([mixed, gram[n:, :n], jnp.broadcast_to(tail, (8, n))], axis=0)
-
-
 def full_path(rows, cols, sketch, tiles, tile_user, tile_item, tile_count, item_owner, packed):
     n = packed.shape[1]
     r = lax.broadcasted_iota(jnp.int32, (n, n), 0)
@@ -409,13 +426,10 @@
 
     fence = lax.optimization_barrier
     far = far_bit
-    whole, *chunks = split_sketch(sketch)
+    flat, whole, chunk = split_sketch(sketch)
     near = spread(whole)
-    crossed = [swap(chunk, "cols", cols, far) for chunk in chunks]
-    gram = lax.dot_general(
-        sketch, sketch, (((0,), (0,)), ((), ())), precision=HIGH, preferred_element_type=F32
-    )
-    packed = pack(gram)
+    crossed = [swap(chunk, "cols", cols, far), swap(whole[2 * CHUNKS[0] :], "cols", cols, far)]
+    packed = packed_gram(flat)
     for bit in near_bits:
         packed = packed + swap(packed, "cols", cols, bit)
     came = swap(packed, "rows", rows, 1)

time: 682 us -> 681 us (level)
  the two profiles are of different devices: /device:TPU:2 before, /device:TPU:0 now
where the time goes in v3:
time: 681 us; the launch traced here: 668 us
  starting transfers between devices  422 us (62%)
  waiting for transfers between devices  98.8 us (15%)
  other arithmetic  59.5 us (9%)
  loops' own time  32.1 us (5%)
  local copies, waits for them, and re-layouts  25.4 us (4%)
  Pallas kernels  15.6 us (2%)
  matrix products  13.5 us (2%)
    ppermute x24, starting transfers between devices, swap(): return lax.ppermute(x, axis, [(i, i ^ bit) for i in range(count)])  422 us
    ppermute x24, waiting for transfers between devices, swap(): return lax.ppermute(x, axis, [(i, i ^ bit) for i in range(count)])  98.8 us
    another operation x6, other arithmetic, full_path(): lower = jnp.linalg.cholesky(gram)  34.2 us
    another operation x1, loops' own time, full_path(): totals = lax.fori_loop(0, tile_count[0], step, totals)  30.1 us
    another operation x5, other arithmetic, full_path(): lax.linalg.triangular_solve(lower, sketch, left_side=False, lower=True, t...  19.8 us
  transfers between devices with their start and end apart: 24, of which 17 were waited for; matrix products, arithmetic and copies ran while one was open for 0% of the time, Pallas kernels for 2%

profile of v3, /device:TPU:0, one launch (start us, length us, event | category | flops | bytes accessed | tf_op | source)
XLA Modules:
  0.0 668.0 jit_solution(5946946557784912023)
XLA Ops:
  0.0 1.6 shard_map.66
  2.2 2.6 collective-permute-start.10
  4.7 1.4 shard_map.67
  7.6 1.6 collective-permute-start.7
  9.9 2.5 shard_map.68
  14.4 5.7 collective-permute-done.10.refs_0_
  20.1 1.8 collective-permute-start.15
  21.9 1.6 collective-permute-start.9
  23.5 3.3 shard_map.69
  27.7 4.0 collective-permute-done.15.refs_0_
  31.7 1.8 collective-permute-start.13
  33.5 1.6 collective-permute-start.14
  35.1 2.6 collective-permute-start.12
  37.7 2.9 shard_map.70
  40.6 4.7 collective-permute-done.12
  46.9 2.8 collective-permute-start.19
  49.8 1.6 collective-permute-start.17
  51.3 3.5 collective-permute-done.17
  54.8 1.4 collective-permute-done.18
  57.7 1.6 collective-permute-start.20
  59.3 1.7 collective-permute-start.22
  61.1 1.7 collective-permute-start.21
  62.9 3.8 shard_map.71
  69.0 5.3 collective-permute-done.23
  74.3 592.9 %conditional.1 = (f32[1,1,256,512]{3,2,1,0:T(8,128)S(1)}) conditional(s32[]{:T(128)} %bitcast.35, (s32[1]{0:T(128)}, f32[264,128]{1,0:T(8,128)S(1)}, f32[1024,256]{1,0:T(8,128)S(1)}, s32[1,8]{1,0:T(1,128)S(1)}, s32[40]{0:T(128)S(1)}, /*index=5*/s32[40]{0:T(128)S(1)}, bf16[40,512,512]{2,1,0:T(8,128)(2,1)}) %tuple.90, (f32[2,96,256]{2,1,0:T(8,128)S(1)}, ...), branch_computations={%region_0.7_spmd, %region_7.8_spmd} | conditional | flops 802537728 | bytes 80229168 | solution.py:483
  75.0 11.7 %cholesky.8 = f32[128,128]{1,0:T(8,128)S(1)} custom-call(f32[128,128]{1,0:T(8,128)S(1)} %cholesky.47), custom_call_target="Cholesky" | custom-call | tf_op jit(solution)/shard_map/cond/branch_0_fun/jit(cholesky)/cholesky | solution.py:351
  87.0 9.8 %custom-call.12 = f32[1,128,128]{1,2,0:T(8,128)S(1)} custom-call(f32[1,128,128]{2,1,0:T(8,128)S(1)} %copy.15), custom_call_target="InvertDiagBlocksLowerTriangular" | custom-call | tf_op jit(solution)/shard_map/cond/branch_0_fun/jit(cholesky)/cholesky | solution.py:351
  97.3 11.7 %cholesky.30 = f32[128,128]{1,0:T(8,128)S(1)} custom-call(f32[128,128]{1,0:T(8,128)S(1)} %convolution_subtract_fusion.1), custom_call_target="Cholesky" | custom-call | tf_op jit(solution)/shard_map/cond/branch_0_fun/jit(cholesky)/cholesky | solution.py:351
  111.4 4.2 while.13
  112.2 1.3 bitcast_dynamic-update-slice_fusion.2
  114.2 1.3 bitcast_dynamic-update-slice_fusion.2
  115.6 19.7 %custom-call.13 = f32[2,128,128]{1,2,0:T(8,128)S(1)} custom-call(f32[2,128,128]{2,1,0:T(8,128)S(1)} %get-tuple-element.277), custom_call_target="InvertDiagBlocksLowerTriangular" | custom-call | tf_op jit(solution)/shard_map/cond/branch_0_fun/triangular_solve | solution.py:352
  137.6 1.6 collective-permute-start.1
  139.2 10.1 %collective-permute-done.1 = bf16[1024,256]{0,1:T(8,128)(2,1)S(1)} collective-permute-done((bf16[1024,256]{0,1:T(8,128)(2,1)S(1)}, bf16[1024,256]{0,1:T(8,128)(2,1)S(1)}, u32[]{:S(2)}, u32[]{:S(2)}) %collective-permute-start.1) | collective-permute-done | bytes 524320 | tf_op jit(solution)/shard_map/cond/branch_0_fun/ppermute | solution.py:29
  151.3 3.1 pad_maximum_fusion
  154.3 2.5 broadcast.96
  156.8 55.1 %while.12 = (s32[]{:T(128)}, f32[8,256,512]{2,1,0:T(8,128)}, s32[]{:T(128)}, s32[40]{0:T(128)S(1)}, s32[8]{0:T(128)S(1)}, /*index=5*/s32[]{:T(128)}, s32[40]{0:T...) while((s32[]{:T(128)}, f32[8,256,512]{2,1,0:T(8,128)}, ...), condition=%wide.region_6.6_spmd, body=%wide.region_5.5_spmd.sunk | while | flops 134348832 | bytes 2884192 | solution.py:374
  165.6 2.1 fusion.30
  176.5 2.1 fusion.30
  187.3 2.1 fusion.30
  198.2 2.1 fusion.30
  209.1 2.2 fusion.30
  211.9 1.9 slice.120
  214.0 26.9 %collective-permute-done.3 = f32[4,256,512]{2,1,0:T(8,128)S(1)} collective-permute-done((f32[4,256,512]{2,1,0:T(8,128)S(1)}, f32[4,256,512]{2,1,0:T(8,128)S(1)}, u32[]{:S(2)}, u32[]{:S(2)}) %collective-permute-start.3) | collective-permute-done | bytes 2097184 | tf_op jit(solution)/shard_map/cond/branch_0_fun/ppermute | solution.py:29
  241.4 94.4 %collective-permute-start.4 = (f32[2,256,512]{2,1,0:T(8,128)S(1)}, f32[2,256,512]{2,1,0:T(8,128)S(1)}, u32[]{:S(2)}, u32[]{:S(2)}) collective-permute-start(f32[2,256,512]{2,1,0:T(8,128)S(1)} %slice.182), channel_id=1, source_target_pairs={{0,8},{4,12},{8,0},{12,4},{16,24},{20,28},{24,16},{28,20},{1,9},{5... | collective-permute-start | bytes 3145736 | tf_op jit(solution)/shard_map/cond/branch_0_fun/ppermute | solution.py:29
  335.8 22.8 %collective-permute-done.4 = f32[2,256,512]{2,1,0:T(8,128)S(1)} collective-permute-done((f32[2,256,512]{2,1,0:T(8,128)S(1)}, f32[2,256,512]{2,1,0:T(8,128)S(1)}, u32[]{:S(2)}, u32[]{:S(2)}) %collective-permute-start.4) | collective-permute-done | bytes 1048608 | tf_op jit(solution)/shard_map/cond/branch_0_fun/ppermute | solution.py:29
  358.8 300.9 %collective-permute-start.5 = (f32[1,256,512]{2,1,0:T(8,128)S(1)}, f32[1,256,512]{2,1,0:T(8,128)S(1)}, u32[]{:S(2)}, u32[]{:S(2)}) collective-permute-start(f32[1,256,512]{2,1,0:T(8,128)S(1)} %slice.184), channel_id=1, source_target_pairs={{0,4},{4,0},{8,12},{12,8},{16,20},{20,16},{24,28},{28,24},{1,5},{5... | collective-permute-start | bytes 1572872 | tf_op jit(solution)/shard_map/cond/branch_0_fun/ppermute | solution.py:29
  659.7 7.2 %collective-permute-done.5 = f32[1,256,512]{2,1,0:T(8,128)S(1)} collective-permute-done((f32[1,256,512]{2,1,0:T(8,128)S(1)}, f32[1,256,512]{2,1,0:T(8,128)S(1)}, u32[]{:S(2)}, u32[]{:S(2)}) %collective-permute-start.5) | collective-permute-done | bytes 524320 | tf_op jit(solution)/shard_map/cond/branch_0_fun/ppermute | solution.py:29
  (128 shorter events, 33.6 us)
Async XLA Ops:
  1.7 8.3 %collective-permute-start.8 = (bf16[512,1024]{1,0:T(8,128)(2,1)S(1)}, bf16[512,1024]{1,0:T(8,128)(2,1)S(1)}, u32[]{:S(2)}, u32[]{:S(2)}) collective-permute-start(bf16[512,1024]{1,0:T(8,128)(2,1)S(1)} %get-tuple-element.226.refs_0_), channel_id=1, source_target_pairs={{0,1},{1,0},{2,3},{3,2},{4,5},{5,4},{6,7},{7,6},{8,9},{9,8},{10,11... | collective-permute-start | bytes 3145736 | tf_op jit(solution)/shard_map/ppermute | solution.py:29
  2.2 17.9 %collective-permute-start.10 = (bf16[320,1024]{1,0:T(8,128)(2,1)S(1)}, bf16[320,1024]{1,0:T(8,128)(2,1)S(1)}, u32[]{:S(2)}, u32[]{:S(2)}) collective-permute-start(bf16[320,1024]{1,0:T(8,128)(2,1)S(1)} %get-tuple-element.231), channel_id=1, source_target_pairs={{0,2},{1,3},{2,0},{3,1},{4,6},{5,7},{6,4},{7,5},{8,10},{9,11},{10,... | collective-permute-start | bytes 1966088 | tf_op jit(solution)/shard_map/ppermute | solution.py:29
  6.2 1.4 collective-permute-start.6
  7.6 5.8 collective-permute-start.7
  9.9 13.6 %copy-start.4 = (s32[1,8]{1,0:T(1,128)S(1)}, s32[1,8]{1,0:T(1,128)}, u32[]{:S(2)}) copy-start(s32[1,8]{1,0:T(1,128)} %param.15) | copy-start | bytes 100
  9.9 13.6 %copy-start.5 = (s32[40]{0:T(128)S(1)}, s32[40]{0:T(128)}, u32[]{:S(2)}) copy-start(s32[40]{0:T(128)} %items.5) | copy-start | bytes 484
  9.9 13.6 %copy-start.6 = (s32[40]{0:T(128)S(1)}, s32[40]{0:T(128)}, u32[]{:S(2)}) copy-start(s32[40]{0:T(128)} %users.5) | copy-start | bytes 484
  20.1 3.4 collective-permute-start.11
  20.1 11.6 %collective-permute-start.15 = (bf16[192,1024]{1,0:T(8,128)(2,1)S(1)}, bf16[192,1024]{1,0:T(8,128)(2,1)S(1)}, u32[]{:S(2)}, u32[]{:S(2)}) collective-permute-start(bf16[192,1024]{1,0:T(8,128)(2,1)S(1)} %slice.148), channel_id=1, source_target_pairs={{0,2},{1,3},{2,0},{3,1},{4,6},{5,7},{6,4},{7,5},{8,10},{9,11},{10,... | collective-permute-start | bytes 1179656 | tf_op jit(solution)/shard_map/ppermute | solution.py:29
  21.9 5.7 collective-permute-start.9
  31.7 5.9 collective-permute-start.16
  31.7 13.6 %collective-permute-start.13 = (bf16[640,256]{1,0:T(8,128)(2,1)S(1)}, bf16[640,256]{1,0:T(8,128)(2,1)S(1)}, u32[]{:S(2)}, u32[]{:S(2)}) collective-permute-start(bf16[640,256]{1,0:T(8,128)(2,1)S(1)} %bitcast.121), channel_id=1, source_target_pairs={{0,4},{4,0},{8,12},{12,8},{16,20},{20,16},{24,28},{28,24},{1,5},{5... | collective-permute-start | bytes 983048 | tf_op jit(solution)/shard_map/ppermute | solution.py:29
  33.5 12.7 %collective-permute-start.14 = (bf16[640,256]{1,0:T(8,128)(2,1)S(1)}, bf16[640,256]{1,0:T(8,128)(2,1)S(1)}, u32[]{:S(2)}, u32[]{:S(2)}) collective-permute-start(bf16[640,256]{1,0:T(8,128)(2,1)S(1)} %bitcast.120), channel_id=1, source_target_pairs={{0,8},{4,12},{8,0},{12,4},{16,24},{20,28},{24,16},{28,20},{1,9},{5... | collective-permute-start | bytes 983048 | tf_op jit(solution)/shard_map/ppermute | solution.py:29
  35.1 10.3 %collective-permute-start.12 = (f32[264,128]{1,0:T(8,128)S(1)}, f32[264,128]{1,0:T(8,128)S(1)}, u32[]{:S(2)}, u32[]{:S(2)}) collective-permute-start(f32[264,128]{1,0:T(8,128)S(1)} %add.136), channel_id=1, source_target_pairs={{0,16},{4,20},{8,24},{12,28},{16,0},{20,4},{24,8},{28,12},{1,17},{... | collective-permute-start | bytes 405512 | tf_op jit(solution)/shard_map/ppermute | solution.py:29
  46.5 9.8 %collective-permute-start.18 = (bf16[704,256]{1,0:T(8,128)(2,1)S(1)}, bf16[704,256]{1,0:T(8,128)(2,1)S(1)}, u32[]{:S(2)}, u32[]{:S(2)}) collective-permute-start(bf16[704,256]{1,0:T(8,128)(2,1)S(1)} %pad_maximum_fusion.2), channel_id=1, source_target_pairs={{0,4},{4,0},{8,12},{12,8},{16,20},{20,16},{24,28},{28,24},{1,5},{5... | collective-permute-start | bytes 1081352 | tf_op jit(solution)/shard_map/ppermute | solution.py:29
  46.9 10.5 %collective-permute-start.19 = (bf16[704,256]{1,0:T(8,128)(2,1)S(1)}, bf16[704,256]{1,0:T(8,128)(2,1)S(1)}, u32[]{:S(2)}, u32[]{:S(2)}) collective-permute-start(bf16[704,256]{1,0:T(8,128)(2,1)S(1)} %pad_maximum_fusion.3), channel_id=1, source_target_pairs={{0,8},{4,12},{8,0},{12,4},{16,24},{20,28},{24,16},{28,20},{1,9},{5... | collective-permute-start | bytes 1081352 | tf_op jit(solution)/shard_map/ppermute | solution.py:29
  49.8 5.1 collective-permute-start.17
  57.5 16.8 %copy-start.1 = (f32[1024,256]{1,0:T(8,128)S(1)}, f32[1024,256]{1,0:T(8,128)}, u32[]{:S(2)}) copy-start(f32[1024,256]{1,0:T(8,128)} %sketch.1) | copy-start | bytes 3145732
  57.7 9.7 %collective-permute-start.20 = (bf16[192,256]{1,0:T(8,128)(2,1)S(1)}, bf16[192,256]{1,0:T(8,128)(2,1)S(1)}, u32[]{:S(2)}, u32[]{:S(2)}) collective-permute-start(bf16[192,256]{1,0:T(8,128)(2,1)S(1)} %bitcast.131), channel_id=1, source_target_pairs={{0,4},{4,0},{8,12},{12,8},{16,20},{20,16},{24,28},{28,24},{1,5},{5... | collective-permute-start | bytes 294920 | tf_op jit(solution)/shard_map/ppermute | solution.py:29
  59.3 8.8 %collective-permute-start.22 = (bf16[320,256]{1,0:T(8,128)(2,1)S(1)}, bf16[320,256]{1,0:T(8,128)(2,1)S(1)}, u32[]{:S(2)}, u32[]{:S(2)}) collective-permute-start(bf16[320,256]{1,0:T(8,128)(2,1)S(1)} %pad_maximum_fusion.5), channel_id=1, source_target_pairs={{0,16},{4,20},{8,24},{12,28},{16,0},{20,4},{24,8},{28,12},{1,17},{... | collective-permute-start | bytes 491528 | tf_op jit(solution)/shard_map/ppermute | solution.py:29
  61.1 6.3 collective-permute-start.21
  68.3 6.0 collective-permute-start.23
  137.6 11.6 %collective-permute-start.1 = (bf16[1024,256]{0,1:T(8,128)(2,1)S(1)}, bf16[1024,256]{0,1:T(8,128)(2,1)S(1)}, u32[]{:S(2)}, u32[]{:S(2)}) collective-permute-start(bf16[1024,256]{0,1:T(8,128)(2,1)S(1)} %pad_maximum_fusion.1), channel_id=1, source_target_pairs={{0,2},{1,3},{2,0},{3,1},{4,6},{5,7},{6,4},{7,5},{8,10},{9,11},{10,... | collective-permute-start | bytes 1572872 | tf_op jit(solution)/shard_map/cond/branch_0_fun/ppermute | solution.py:29
  139.2 10.1 %collective-permute-start = (bf16[1024,256]{0,1:T(8,128)(2,1)S(1)}, bf16[1024,256]{0,1:T(8,128)(2,1)S(1)}, u32[]{:S(2)}, u32[]{:S(2)}) collective-permute-start(bf16[1024,256]{0,1:T(8,128)(2,1)S(1)} %pad_maximum_fusion.1), channel_id=1, source_target_pairs={{0,1},{1,0},{2,3},{3,2},{4,5},{5,4},{6,7},{7,6},{8,9},{9,8},{10,11... | collective-permute-start | bytes 1572872 | tf_op jit(solution)/shard_map/cond/branch_0_fun/ppermute | solution.py:29
  149.2 2.0 collective-permute-start.2
  149.2 0.8 copy-start.3
  211.9 28.9 %copy-start = (f32[8,256,512]{2,1,0:T(8,128)S(1)}, f32[8,256,512]{2,1,0:T(8,128)}, u32[]{:S(2)}) copy-start(f32[8,256,512]{2,1,0:T(8,128)} %get-tuple-element.173) | copy-start | bytes 12582916 | tf_op jit(solution)/shard_map/cond
  213.8 27.0 %collective-permute-start.3 = (f32[4,256,512]{2,1,0:T(8,128)S(1)}, f32[4,256,512]{2,1,0:T(8,128)S(1)}, u32[]{:S(2)}, u32[]{:S(2)}) collective-permute-start(f32[4,256,512]{2,1,0:T(8,128)S(1)} %slice.120), channel_id=1, source_target_pairs={{0,16},{4,20},{8,24},{12,28},{16,0},{20,4},{24,8},{28,12},{1,17},{... | collective-permute-start | bytes 6291464 | tf_op jit(solution)/shard_map/cond/branch_0_fun/ppermute | solution.py:29
  241.4 117.2 %collective-permute-start.4 = (f32[2,256,512]{2,1,0:T(8,128)S(1)}, f32[2,256,512]{2,1,0:T(8,128)S(1)}, u32[]{:S(2)}, u32[]{:S(2)}) collective-permute-start(f32[2,256,512]{2,1,0:T(8,128)S(1)} %slice.182), channel_id=1, source_target_pairs={{0,8},{4,12},{8,0},{12,4},{16,24},{20,28},{24,16},{28,20},{1,9},{5... | collective-permute-start | bytes 3145736 | tf_op jit(solution)/shard_map/cond/branch_0_fun/ppermute | solution.py:29
  358.8 308.1 %collective-permute-start.5 = (f32[1,256,512]{2,1,0:T(8,128)S(1)}, f32[1,256,512]{2,1,0:T(8,128)S(1)}, u32[]{:S(2)}, u32[]{:S(2)}) collective-permute-start(f32[1,256,512]{2,1,0:T(8,128)S(1)} %slice.184), channel_id=1, source_target_pairs={{0,4},{4,0},{8,12},{12,8},{16,20},{20,16},{24,28},{28,24},{1,5},{5... | collective-permute-start | bytes 1572872 | tf_op jit(solution)/shard_map/cond/branch_0_fun/ppermute | solution.py:29
  667.2 0.8 copy-start.2
